TPU v7x, 512 devices: a whole 4x4x16 slice. The times are simulated.
512 devices in a mesh: rows: 512 (over y, z, x, core).
Axes of the slice: x: 4, y: 4, z: 16, core: 2. Of those that a mesh axis runs over, the one named last changes fastest.
Arguments:
- right_side: float32 [64, 131072], P(None, 'rows'), may hold values from -6 to 6
- blocks: float32 [7, 64, 131072], P(None, None, 'rows'), may hold values from -0.18898223 to 0.18898223
- cols: int32 [7, 2048], P(None, 'rows'), may hold values from 0 to 2047, as said below
Outputs:
- update: float32 [64, 131072], P(None, 'rows')
- new_residual: float32 [64, 131072], P(None, 'rows')
Inputs may be any that keep to these rules, and one draw needn't show every extreme that they name: For block row i, cols[0, i] = i, cols[1, i] and cols[2, i] are i + 1 and i - 1, cols[3, i] and cols[4, i] are i + 1 and i - 1, and cols[5, i], cols[6, i] lie within 1 of i, all modulo 2048.
All inputs are finite; a program needn't handle non-finite values.
Results may differ from a plain program's by a relative error of at most 0.00026.
Values sent between devices are 32-bit elements; how exact they have to be, the bound alone decides.
No kernel may reach another device: no remote copies, remote signals or barrier semaphores. Data moves between devices by JAX's collectives and lax.ppermute only.
A program may use at most 64 MiB of HBM per device.

v0:
```python
import jax
import jax.numpy as jnp
from jax import lax
from jax.sharding import PartitionSpec as P

S = 4


SCALE = 1.25


def extended_2(cells, sides, width):
    for axis, dim in sides:
        count = lax.axis_size(axis)
        head = lax.slice_in_dim(cells, 0, width, axis=dim)
        tail = lax.slice_in_dim(cells, cells.shape[dim] - width, cells.shape[dim], axis=dim)
        cells = jnp.concatenate(
            [
                lax.ppermute(tail, axis, [(i, (i + 1) % count) for i in range(count)]),
                cells,
                lax.ppermute(head, axis, [((i + 1) % count, i) for i in range(count)]),
            ],
            axis=dim,
        )
    return cells


def multiply(vector, blocks, local_cols):
    sources = vector.shape[0]
    width = blocks.shape[1]
    shaped = vector.reshape(sources, -1, width)
    count = local_cols.shape[1]
    total = jnp.zeros((sources, count, width), jnp.float32)
    for slot in range(local_cols.shape[0]):
        picked = jnp.take(shaped, local_cols[slot], axis=1)
        matrix = blocks[slot].reshape(width, count, width)
        total = total + jnp.einsum("cir,aic->air", matrix, picked, precision=lax.Precision.HIGHEST)
    return total.reshape(sources, count * width)


def inner(left, right):
    return lax.dot_general(
        left,
        right,
        (((1,), (1,)), ((), ())),
        precision=lax.Precision.HIGHEST,
        preferred_element_type=jnp.float32,
    )


def shards(right_side, blocks, cols):
    devices = lax.axis_size("rows")
    position = lax.axis_index("rows")
    local_blocks = cols.shape[1]
    width = blocks.shape[1]
    sources = right_side.shape[0]
    reach = local_blocks // 4
    total_blocks = local_blocks * devices
    first_block = position * local_blocks
    powers = [right_side]
    shifted = jnp.mod(cols - (first_block - reach), total_blocks)
    current = right_side
    for step in range(S):
        extended = extended_2(current, (("rows", 1),), reach * width)
        current = SCALE * multiply(extended, blocks, shifted)
        powers.append(current)
    stack = jnp.concatenate(powers, axis=0)
    order = stack.shape[0]
    gram = lax.psum(inner(stack, stack), "rows")
    mixing = (
        jnp.eye(order, order - sources, dtype=jnp.float32)
        + jnp.eye(order, order - sources, k=-sources, dtype=jnp.float32) / SCALE
    )
    high = lax.Precision.HIGHEST
    folded = jnp.dot(mixing.T, gram, precision=high, preferred_element_type=jnp.float32)
    normal = jnp.dot(folded, mixing, precision=high, preferred_element_type=jnp.float32)
    target = folded[:, :sources]
    factor = jnp.linalg.cholesky(normal)
    coeff = jax.scipy.linalg.cho_solve((factor, True), target)
    dims = (((0,), (0,)), ((), ()))
    update = lax.dot_general(
        coeff, stack[: order - sources], dims, precision=high, preferred_element_type=jnp.float32
    )
    images = stack[: order - sources] + stack[sources:] / SCALE
    new_residual = right_side - lax.dot_general(
        coeff, images, dims, precision=high, preferred_element_type=jnp.float32
    )
    return (update, new_residual)


def solution(mesh):
    in_specs = (P(None, "rows"), P(None, None, "rows"), P(None, "rows"))
    out_specs = (P(None, "rows"), P(None, "rows"))
    return jax.shard_map(shards, mesh=mesh, in_specs=in_specs, out_specs=out_specs, check_vma=False)
```

profile of v0, /device:TPU:1, one launch (start us, length us, event | category | flops | bytes accessed | tf_op | source)
XLA Modules:
  0.0 626.5 jit_solution(9474320586029394011)
XLA Ops:
  7.2 0.9 fusion.222
  8.1 4.6 collective-permute-start
  12.7 6.2 collective-permute-start.1
  19.4 1.1 fusion.218
  21.6 0.6 gather_fusion
  22.2 0.6 gather_fusion.1
  22.7 0.6 gather_fusion.2
  23.3 0.6 gather_fusion.3
  23.9 0.6 gather_fusion.4
  24.4 0.6 gather_fusion.5
  25.0 0.6 gather_fusion.6
  28.2 1.9 collective-permute-start.2
  30.1 10.2 %collective-permute-start.3 = (f32[64,64]{1,0:T(8,128)S(1)}, f32[64,64]{1,0:T(8,128)S(1)}, u32[]{:S(2)}, u32[]{:S(2)}) collective-permute-start(f32[64,64]{1,0:T(8,128)S(1)} %get-tuple-element.52), channel_id=1, source_target_pairs={{1,0},{2,1},{3,2},{4,3},{5,4},{6,5},{7,6},{8,7},{9,8},{10,9},{11,1... | collective-permute-start | bytes 49160 | tf_op jit(solution)/shard_map/ppermute | solution.py:21
  40.3 0.8 collective-permute-done.3
  41.3 0.6 gather_fusion.7
  41.9 0.6 gather_fusion.8
  42.5 0.6 gather_fusion.9
  43.0 0.6 gather_fusion.10
  43.6 0.6 gather_fusion.11
  44.2 0.6 gather_fusion.12
  44.7 0.6 gather_fusion.13
  47.9 1.9 collective-permute-start.4
  49.8 9.8 %collective-permute-start.5 = (f32[64,64]{1,0:T(8,128)S(1)}, f32[64,64]{1,0:T(8,128)S(1)}, u32[]{:S(2)}, u32[]{:S(2)}) collective-permute-start(f32[64,64]{1,0:T(8,128)S(1)} %get-tuple-element.50), channel_id=1, source_target_pairs={{1,0},{2,1},{3,2},{4,3},{5,4},{6,5},{7,6},{8,7},{9,8},{10,9},{11,1... | collective-permute-start | bytes 49160 | tf_op jit(solution)/shard_map/ppermute | solution.py:21
  59.6 0.8 collective-permute-done.5
  60.7 0.6 gather_fusion.14
  61.3 0.6 gather_fusion.15
  67.3 1.9 collective-permute-start.6
  69.2 10.0 %collective-permute-start.7 = (f32[64,64]{1,0:T(8,128)S(1)}, f32[64,64]{1,0:T(8,128)S(1)}, u32[]{:S(2)}, u32[]{:S(2)}) collective-permute-start(f32[64,64]{1,0:T(8,128)S(1)} %get-tuple-element.40), channel_id=1, source_target_pairs={{1,0},{2,1},{3,2},{4,3},{5,4},{6,5},{7,6},{8,7},{9,8},{10,9},{11,1... | collective-permute-start | bytes 49160 | tf_op jit(solution)/shard_map/ppermute | solution.py:21
  79.2 0.6 collective-permute-done.7
  80.1 0.6 gather_fusion.21
  83.5 0.6 gather_fusion.27
  86.6 1.5 fusion.223
  88.1 464.4 %all-reduce.3.cloned.1.call-done = f32[320,320]{1,0:T(8,128)} async-done(((f32[320,320]{1,0:T(8,128)}), f32[320,320]{1,0:T(8,128)}) %all-reduce.3.cloned.1.call-update) | async-done | bytes 409616 | tf_op jit(solution)/shard_map/psum | solution.py:69
  552.5 2.2 fusion.9
  554.7 0.9 fusion.8
  555.8 11.7 %cholesky.50 = f32[128,128]{1,0:T(8,128)S(1)} custom-call(f32[128,128]{1,0:T(8,128)S(1)} %cholesky.118), custom_call_target="Cholesky" | custom-call | tf_op jit(solution)/shard_map/jit(cholesky)/cholesky | solution.py:78
  567.6 9.8 %custom-call.18 = f32[1,128,128]{1,2,0:T(8,128)S(1)} custom-call(f32[1,128,128]{2,1,0:T(8,128)S(1)} %get-tuple-element.38), custom_call_target="InvertDiagBlocksLowerTriangular" | custom-call | tf_op jit(solution)/shard_map/jit(cholesky)/cholesky | solution.py:78
  577.9 11.9 %cholesky.105 = f32[128,128]{1,0:T(8,128)S(1)} custom-call(f32[128,128]{1,0:T(8,128)S(1)} %convolution_subtract_fusion), custom_call_target="Cholesky" | custom-call | tf_op jit(solution)/shard_map/jit(cholesky)/cholesky | solution.py:78
  589.8 0.7 compare_reduce_fusion
  590.6 0.6 compare_reduce_fusion.1
  592.7 4.1 while.1
  592.7 0.6 fusion.237
  593.3 1.4 bitcast_dynamic-update-slice_fusion.2
  594.7 0.6 fusion.237
  595.3 1.4 bitcast_dynamic-update-slice_fusion.2
  596.8 19.7 %custom-call.19 = f32[2,128,128]{1,2,0:T(8,128)S(1)} custom-call(f32[2,128,128]{2,1,0:T(8,128)S(1)} %get-tuple-element.10), custom_call_target="InvertDiagBlocksLowerTriangular" | custom-call | tf_op jit(solution)/shard_map/jit(_cho_solve)/triangular_solve | solution.py:79
  617.9 0.9 convolution_subtract_fusion.1
  618.8 0.9 fusion.179
  (122 shorter events, 20.1 us)
Async XLA Ops:
  7.2 545.4 %all-reduce.3.cloned.1.call-start = ((), (), s32[]{:S(2)}) async-start(), calls=%async_computation | async-start | bytes 983040 | tf_op jit(solution)/shard_map/psum | solution.py:69
  7.2 11.7 %copy-start.1 = (s32[7,4]{0,1:T(4,128)S(1)}, s32[7,4]{0,1:T(4,128)}, u32[]{:S(2)}) copy-start(s32[7,4]{0,1:T(4,128)} %param.7) | copy-start | bytes 340
  8.1 11.2 %copy-start = (f32[64,256]{1,0:T(8,128)S(1)}, f32[64,256]{1,0:T(8,128)}, u32[]{:S(2)}) copy-start(f32[64,256]{1,0:T(8,128)} %param.5) | copy-start | bytes 196612
  8.1 13.3 %collective-permute-start = (f32[64,64]{1,0:T(8,128)S(1)}, f32[64,64]{1,0:T(8,128)S(1)}, u32[]{:S(2)}, u32[]{:S(2)}) collective-permute-start(f32[64,64]{1,0:T(8,128)S(1)} %get-tuple-element.53), channel_id=1, source_target_pairs={{0,1},{1,2},{2,3},{3,4},{4,5},{5,6},{6,7},{7,8},{8,9},{9,10},{10,1... | collective-permute-start | bytes 49160 | tf_op jit(solution)/shard_map/ppermute | solution.py:19
  12.7 8.6 %collective-permute-start.1 = (f32[64,64]{1,0:T(8,128)S(1)}, f32[64,64]{1,0:T(8,128)S(1)}, u32[]{:S(2)}, u32[]{:S(2)}) collective-permute-start(f32[64,64]{1,0:T(8,128)S(1)} %get-tuple-element.54), channel_id=1, source_target_pairs={{1,0},{2,1},{3,2},{4,3},{5,4},{6,5},{7,6},{8,7},{9,8},{10,9},{11,1... | collective-permute-start | bytes 49160 | tf_op jit(solution)/shard_map/ppermute | solution.py:21
  28.2 12.1 %collective-permute-start.2 = (f32[64,64]{1,0:T(8,128)S(1)}, f32[64,64]{1,0:T(8,128)S(1)}, u32[]{:S(2)}, u32[]{:S(2)}) collective-permute-start(f32[64,64]{1,0:T(8,128)S(1)} %get-tuple-element.51), channel_id=1, source_target_pairs={{0,1},{1,2},{2,3},{3,4},{4,5},{5,6},{6,7},{7,8},{8,9},{9,10},{10,1... | collective-permute-start | bytes 49160 | tf_op jit(solution)/shard_map/ppermute | solution.py:19
  30.1 11.0 %collective-permute-start.3 = (f32[64,64]{1,0:T(8,128)S(1)}, f32[64,64]{1,0:T(8,128)S(1)}, u32[]{:S(2)}, u32[]{:S(2)}) collective-permute-start(f32[64,64]{1,0:T(8,128)S(1)} %get-tuple-element.52), channel_id=1, source_target_pairs={{1,0},{2,1},{3,2},{4,3},{5,4},{6,5},{7,6},{8,7},{9,8},{10,9},{11,1... | collective-permute-start | bytes 49160 | tf_op jit(solution)/shard_map/ppermute | solution.py:21
  47.9 11.8 %collective-permute-start.4 = (f32[64,64]{1,0:T(8,128)S(1)}, f32[64,64]{1,0:T(8,128)S(1)}, u32[]{:S(2)}, u32[]{:S(2)}) collective-permute-start(f32[64,64]{1,0:T(8,128)S(1)} %get-tuple-element.49), channel_id=1, source_target_pairs={{0,1},{1,2},{2,3},{3,4},{4,5},{5,6},{6,7},{7,8},{8,9},{9,10},{10,1... | collective-permute-start | bytes 49160 | tf_op jit(solution)/shard_map/ppermute | solution.py:19
  49.8 10.7 %collective-permute-start.5 = (f32[64,64]{1,0:T(8,128)S(1)}, f32[64,64]{1,0:T(8,128)S(1)}, u32[]{:S(2)}, u32[]{:S(2)}) collective-permute-start(f32[64,64]{1,0:T(8,128)S(1)} %get-tuple-element.50), channel_id=1, source_target_pairs={{1,0},{2,1},{3,2},{4,3},{5,4},{6,5},{7,6},{8,7},{9,8},{10,9},{11,1... | collective-permute-start | bytes 49160 | tf_op jit(solution)/shard_map/ppermute | solution.py:21
  67.3 11.9 %collective-permute-start.6 = (f32[64,64]{1,0:T(8,128)S(1)}, f32[64,64]{1,0:T(8,128)S(1)}, u32[]{:S(2)}, u32[]{:S(2)}) collective-permute-start(f32[64,64]{1,0:T(8,128)S(1)} %get-tuple-element.39), channel_id=1, source_target_pairs={{0,1},{1,2},{2,3},{3,4},{4,5},{5,6},{6,7},{7,8},{8,9},{9,10},{10,1... | collective-permute-start | bytes 49160 | tf_op jit(solution)/shard_map/ppermute | solution.py:19
  69.2 10.7 %collective-permute-start.7 = (f32[64,64]{1,0:T(8,128)S(1)}, f32[64,64]{1,0:T(8,128)S(1)}, u32[]{:S(2)}, u32[]{:S(2)}) collective-permute-start(f32[64,64]{1,0:T(8,128)S(1)} %get-tuple-element.40), channel_id=1, source_target_pairs={{1,0},{2,1},{3,2},{4,3},{5,4},{6,5},{7,6},{8,7},{9,8},{10,9},{11,1... | collective-permute-start | bytes 49160 | tf_op jit(solution)/shard_map/ppermute | solution.py:21
Sparse Core Ops, SparseCore 0:
  88.2 464.2 all-reduce.2
where the time goes:
time: 628 us; the launch traced here: 627 us
  waiting for transfers between devices  467 us (74%)
  other arithmetic  55.1 us (9%)
  starting transfers between devices  46.5 us (7%)
  local copies, waits for them, and re-layouts  24.6 us (4%)
  matrix products  17.1 us (3%)
  between operations  16.4 us (3%)
    psum x1, waiting for transfers between devices, shards(): gram = lax.psum(inner(stack, stack), 'rows')  464 us
    ppermute x4, starting transfers between devices, extended_2(): lax.ppermute(head, axis, [((i + 1) % count, i) for i in range(count)])  36.1 us
    another operation x7, other arithmetic, shards(): factor = jnp.linalg.cholesky(normal)  34.9 us
    another operation x3, other arithmetic, shards(): coeff = jax.scipy.linalg.cho_solve((factor, True), target)  19.7 us
    gather x28, local copies, waits for them, and re-layouts, multiply(): picked = jnp.take(shaped, local_cols[slot], axis=1)  15.6 us
  transfers between devices with their start and end apart: 9, of which 4 were waited for; matrix products, arithmetic and copies ran while one was open for 0% of the time, Pallas kernels for 0%

commit v1 on v0

v1 whole, which is shorter than its diff:
```python
import functools

import jax
import jax.numpy as jnp
from jax import lax
from jax.experimental import pallas as pl
from jax.experimental.pallas import tpu as pltpu
from jax.sharding import Mesh, PartitionSpec as P

SCALE = 1.25
S = 4
BS = 64
HIGH = lax.Precision.HIGHEST

VMEM = pl.BlockSpec(memory_space=pltpu.VMEM)
SMEM = pl.BlockSpec(memory_space=pltpu.SMEM)


def dot(a, b, dims):
    return lax.dot_general(a, b, (dims, ((), ())), precision=HIGH, preferred_element_type=jnp.float32)


def pack_kernel(total_blocks, cols_ref, right_ref, blocks_ref, out_ref):
    width = right_ref.shape[1]
    lane = lax.broadcasted_iota(jnp.int32, (1, width), 1) // BS
    minus = blocks_ref[2] + blocks_ref[4]
    zero = blocks_ref[0]
    plus = blocks_ref[1] + blocks_ref[3]
    for slot in (5, 6):
        offset = jnp.zeros((1, width), jnp.int32)
        for row in range(width // BS):
            delta = cols_ref[slot, row] - cols_ref[0, row]
            delta = jnp.where(delta > 1, delta - total_blocks, delta)
            delta = jnp.where(delta < -1, delta + total_blocks, delta)
            offset = jnp.where(lane == row, delta, offset)
        matrix = blocks_ref[slot]
        minus = minus + jnp.where(offset == -1, matrix, 0.0)
        zero = zero + jnp.where(offset == 0, matrix, 0.0)
        plus = plus + jnp.where(offset == 1, matrix, 0.0)
    out_ref[0:64, :] = minus
    out_ref[64:128, :] = zero
    out_ref[128:192, :] = plus
    out_ref[192:256, :] = right_ref[...]


def basis_kernel(cols_ref, own_ref, pair_ref, other_ref, sums_ref, stack_ref, ext_ref, band_ref):
    even = lax.rem(cols_ref[0, 0] // 4, 2) == 0

    @pl.when(even)
    def _():
        ext_ref[:, 0:256] = other_ref[...]
        ext_ref[:, 512:768] = pair_ref[...]

    @pl.when(jnp.logical_not(even))
    def _():
        ext_ref[:, 0:256] = pair_ref[...]
        ext_ref[:, 512:768] = other_ref[...]

    ext_ref[:, 256:512] = own_ref[...]
    left = lax.broadcasted_iota(jnp.int32, (BS, 128), 1) < BS
    for p in range(6):
        at = slice(128 * p, 128 * (p + 1))
        minus, zero, plus = ext_ref[0:64, at], ext_ref[64:128, at], ext_ref[128:192, at]
        band_ref[p, 0:64, :] = jnp.where(left, minus, 0.0)
        band_ref[p, 64:128, :] = jnp.where(left, zero, minus)
        band_ref[p, 128:192, :] = jnp.where(left, plus, zero)
        band_ref[p, 192:256, :] = jnp.where(left, 0.0, plus)
    current = ext_ref[192:256, :]
    first = 0
    own = [current[:, 256:512]]
    images = []
    for step, (low, high) in enumerate(((0, 6), (1, 5), (1, 5), (2, 4))):
        rolled = pltpu.roll(current, 64, 1)
        parts = []
        for p in range(low, high):
            at = 128 * (p - first)
            if at + 256 <= rolled.shape[1]:
                window = rolled[:, at : at + 256]
            else:
                window = jnp.concatenate([rolled[:, at:], rolled[:, :128]], axis=1)
            parts.append(dot(window, band_ref[p], ((1,), (0,))))
        product = jnp.concatenate(parts, axis=1)
        inner = product[:, 256 - 128 * low : 512 - 128 * low]
        images.append(own[step] + inner)
        current = SCALE * product
        first = low
        own.append(SCALE * inner)
    w = jnp.concatenate(images, axis=0)
    stack_ref[:, 0:256] = jnp.concatenate(own[:S], axis=0)
    stack_ref[:, 256:512] = w
    gram = dot(w, jnp.concatenate([own[0], w], axis=0), ((1,), (1,)))
    sums_ref[0:64, :] = gram[0:64, 0:128]
    sums_ref[64:128, :] = gram[64:128, 0:128]
    sums_ref[128:192, :] = gram[128:192, 0:128]
    sums_ref[192:256, :] = gram[128:192, 128:256]
    sums_ref[256:320, :] = gram[192:256, 0:128]
    sums_ref[320:384, :] = gram[192:256, 128:256]
    sums_ref[384:448, :] = jnp.concatenate([gram[64:128, 128:192], gram[192:256, 256:320]], axis=1)
    sums_ref[448:512, :] = jnp.zeros((64, 128), jnp.float32)


def total_kernel(copies, in_ref, out_ref):
    total = in_ref[0]
    for k in range(1, in_ref.shape[0]):
        total = total + in_ref[k]
    for k in range(copies):
        out_ref[k] = total


def eliminate(block):
    rows = lax.broadcasted_iota(jnp.int32, (BS, 1), 0)
    for k in range(BS):
        pivot_row = block[k : k + 1, :] / block[k : k + 1, k : k + 1]
        factor = jnp.where(rows == k, 0.0, block[:, k : k + 1])
        block = jnp.where(rows == k, pivot_row, block - factor * pivot_row)
    return block


def solve_kernel(sums_ref, stack_ref, right_ref, update_ref, residual_ref):
    u = [sums_ref[64 * k : 64 * (k + 1), :] for k in range(7)]
    t = [u[0][:, 0:64], u[1][:, 0:64], u[2][:, 0:64], u[4][:, 0:64]]
    n = {}
    n[0, 0] = u[0][:, 64:128]
    n[1, 0] = u[1][:, 64:128]
    n[1, 1] = u[6][:, 0:64]
    n[2, 0] = u[2][:, 64:128]
    n[2, 1] = u[3][:, 0:64]
    n[2, 2] = u[3][:, 64:128]
    n[3, 0] = u[4][:, 64:128]
    n[3, 1] = u[5][:, 0:64]
    n[3, 2] = u[5][:, 64:128]
    n[3, 3] = u[6][:, 64:128]
    done = []
    for k in range(S):
        below = [n[i, k] for i in range(k + 1, S)]
        wide = [n[k, k]] + [b.T for b in below] + [t[k]]
        wide = eliminate(jnp.concatenate(wide, axis=1))
        done.append(wide)
        for i in range(k + 1, S):
            change = dot(n[i, k], wide, ((1,), (0,)))
            for j in range(k + 1, i + 1):
                n[i, j] = n[i, j] - change[:, 64 * (j - k) : 64 * (j - k + 1)]
            t[i] = t[i] - change[:, 64 * (S - k) : 64 * (S - k + 1)]
    x = [None] * S
    for k in range(S - 1, -1, -1):
        x[k] = done[k][:, 64 * (S - k) : 64 * (S - k + 1)]
        for j in range(k + 1, S):
            x[k] = x[k] - dot(done[k][:, 64 * (j - k) : 64 * (j - k + 1)], x[j], ((1,), (0,)))
    coeff = jnp.concatenate(x, axis=0)
    both = dot(coeff, stack_ref[...], ((0,), (0,)))
    update_ref[...] = both[:, 0:256]
    residual_ref[...] = right_ref[...] - both[:, 256:512]


def call(kernel, outs, in_specs, scratch=(), name=None):
    shapes = [jax.ShapeDtypeStruct(s, jnp.float32) for s in outs]
    specs = [VMEM] * len(outs)
    return pl.pallas_call(
        kernel,
        out_shape=shapes if len(outs) > 1 else shapes[0],
        in_specs=in_specs,
        out_specs=specs if len(outs) > 1 else specs[0],
        scratch_shapes=list(scratch),
        name=name,
        compiler_params=pltpu.CompilerParams(vmem_limit_bytes=48 * 1024 * 1024),
    )


def pack(cols, right_side, blocks, total_blocks):
    kernel = functools.partial(pack_kernel, total_blocks)
    return call(kernel, [(256, 256)], [SMEM, VMEM, VMEM], name="pack")(cols, right_side, blocks)


def basis(cols, own, pair, other):
    scratch = (pltpu.VMEM((256, 768), jnp.float32), pltpu.VMEM((6, 256, 128), jnp.float32))
    return call(basis_kernel, [(512, 128), (256, 512)], [SMEM, VMEM, VMEM, VMEM], scratch, name="basis")(cols, own, pair, other)


def total(parts, copies):
    kernel = functools.partial(total_kernel, copies)
    return call(kernel, [(copies,) + parts.shape[1:]], [VMEM], name="total")(parts)


def solve(sums, stack, right_side):
    return call(solve_kernel, [(64, 256), (64, 256)], [VMEM, VMEM, VMEM], name="solve")(sums, stack, right_side)


AXES = ("y", "z", "x", "core")
PLANE = ("y", "x", "core")


def shards(right_side, blocks, cols):
    devices = lax.axis_size(AXES)
    own = pack(cols, right_side, blocks, cols.shape[1] * devices)
    pair = lax.ppermute(own, AXES, [(i, i ^ 1) for i in range(devices)])
    other = lax.ppermute(own, AXES, [(i, ((i - 1) ^ 1) + 1 if i else devices - 1) if i < devices - 1 else (i, 0) for i in range(devices)])
    sums, stack = basis(cols, own, pair, other)
    parts = lax.all_to_all(sums.reshape(32, 16, 128), PLANE, 0, 0)
    parts = lax.all_to_all(total(parts, 16), "z", 0, 0)
    sums = lax.all_to_all(total(parts, 32), PLANE, 0, 0)
    return tuple(solve(sums.reshape(512, 128), stack, right_side))


def solution(mesh):
    grid = Mesh(mesh.devices.reshape(4, 16, 4, 2), AXES)
    in_specs = (P(None, AXES), P(None, None, AXES), P(None, AXES))
    out_specs = (P(None, AXES), P(None, AXES))
    return jax.shard_map(shards, mesh=grid, in_specs=in_specs, out_specs=out_specs, check_vma=False)
```

time: 628 us -> 101 us (0.16)
  waiting for transfers between devices: 467 us -> 1.13 us
  other arithmetic: 55.1 us -> 0 us
  blocking collectives: 0 us -> 48.3 us
  Pallas kernels: 0 us -> 28.6 us
  starting transfers between devices: 46.5 us -> 18.9 us
  local copies, waits for them, and re-layouts: 24.6 us -> 2.63 us
  matrix products: 17.1 us -> 0 us
  between operations: 16.4 us -> 0.69 us
    psum x1 -> x0, waiting for transfers between devices: 464 us -> none  [shards(): gram = lax.psum(inner(stack, stack), 'rows')]
    another operation x10 -> x0, other arithmetic: 54.6 us -> none  [the longest x7 34.9 us: shards(): factor = jnp.linalg.cholesky(normal)]
    all_to_all x0 -> x3, blocking collectives: none -> 48.3 us  [the longest x1 20.4 us: shards(): parts = lax.all_to_all(total(parts, 16), 'z', 0, 0)]
    pallas_call x0 -> x5, Pallas kernels: none -> 28.6 us  [the longest x1 25.1 us: solve(): call(solve_kernel, [(64, 256), (64, 256)], [VMEM, VMEM, VMEM], name='solve')]
    ppermute x8 -> x2, starting transfers between devices: 46.5 us -> 18.9 us  [the longest x1 14.4 us: shards(): pair = lax.ppermute(own, AXES, [(i, i ^ 1) for i in range(devices)])]
    gather x28 -> x0, local copies, waits for them, and re-layouts: 15.6 us -> none  [multiply(): picked = jnp.take(shaped, local_cols[slot], axis=1)]
    dot_general x33 -> x0, matrix products: 15.3 us -> none  [the longest x28 8.94 us: multiply(): jnp.einsum('cir,aic->air', matrix, picked, precision=lax.Precision.HIGHEST)]
  transfers between devices with their start and end apart: 9 -> 2, of which waited for: 4 -> 1; matrix products, arithmetic and copies ran while one was open for 0% -> 0% of each run, Pallas kernels for 0% -> 0%
where the time goes in v1:
time: 101 us; the launch traced here: 100 us
  blocking collectives  48.3 us (48%)
  Pallas kernels  28.6 us (28%)
  starting transfers between devices  18.9 us (19%)
  local copies, waits for them, and re-layouts  2.63 us (3%)
  waiting for transfers between devices  1.13 us (1%)
    pallas_call x1, Pallas kernels, solve(): call(solve_kernel, [(64, 256), (64, 256)], [VMEM, VMEM, VMEM], name='solve')  25.1 us
    all_to_all x1, blocking collectives, shards(): parts = lax.all_to_all(total(parts, 16), 'z', 0, 0)  20.4 us
    all_to_all x1, blocking collectives, shards(): sums = lax.all_to_all(total(parts, 32), PLANE, 0, 0)  15.3 us
    ppermute x1, starting transfers between devices, shards(): pair = lax.ppermute(own, AXES, [(i, i ^ 1) for i in range(devices)])  14.4 us
    all_to_all x1, blocking collectives, shards(): parts = lax.all_to_all(sums.reshape(32, 16, 128), PLANE, 0, 0)  12.6 us
    ppermute x1, starting transfers between devices, shards(): lax.ppermute(own, AXES, [(i, (i - 1 ^ 1) + 1 if i else devices - 1) if i...  4.5 us
    pallas_call x1, Pallas kernels, basis(): call(basis_kernel, [(512, 128), (256, 512)], [SMEM, VMEM, VMEM, VMEM], sc...  2.73 us
    unnamed x7, local copies, waits for them, and re-layouts  2.63 us
  transfers between devices with their start and end apart: 2, of which 1 were waited for; matrix products, arithmetic and copies ran while one was open for 0% of the time, Pallas kernels for 0%

profile of v1, /device:TPU:1, one launch (start us, length us, event | category | flops | bytes accessed | tf_op | source)
XLA Modules:
  0.0 100.2 jit_solution(9077205249307940656)
XLA Ops:
  0.6 0.8 copy.6.cols_ref
  1.4 0.0 copy-start
  1.4 1.0 %copy-done = f32[7,64,256]{2,1,0:T(8,128)S(1)} copy-done((f32[7,64,256]{2,1,0:T(8,128)S(1)}, f32[7,64,256]{2,1,0:T(8,128)}, u32[]{:S(2)}) %copy-start) | copy-done | bytes 458776
  2.4 0.0 copy-start.1
  2.4 0.8 copy-done.1
  3.3 0.6 pack.1.own_ref
  3.9 4.5 %collective-permute-start.1 = (f32[256,256]{1,0:T(8,128)S(1)}, f32[256,256]{1,0:T(8,128)S(1)}, u32[]{:S(2)}, u32[]{:S(2)}) collective-permute-start(f32[256,256]{1,0:T(8,128)S(1)} %pack.1.own_ref), channel_id=1, source_target_pairs={{0,511},{1,2},{2,1},{3,4},{4,3},{5,6},{6,5},{7,8},{8,7},{9,10},{10... | collective-permute-start | bytes 786440 | tf_op jit(solution)/shard_map/ppermute | solution.py:196
  8.4 14.4 %collective-permute-start = (f32[256,256]{1,0:T(8,128)S(1)}, f32[256,256]{1,0:T(8,128)S(1)}, u32[]{:S(2)}, u32[]{:S(2)}) collective-permute-start(f32[256,256]{1,0:T(8,128)S(1)} %pack.1.own_ref), channel_id=1, source_target_pairs={{0,1},{1,0},{2,3},{3,2},{4,5},{5,4},{6,7},{7,6},{8,9},{9,8},{10,11... | collective-permute-start | bytes 786440 | tf_op jit(solution)/shard_map/ppermute | solution.py:195
  22.8 0.0 collective-permute-done.1.other_ref
  22.8 1.1 %collective-permute-done.pair_ref = f32[256,256]{1,0:T(8,128)S(1)} collective-permute-done((f32[256,256]{1,0:T(8,128)S(1)}, f32[256,256]{1,0:T(8,128)S(1)}, u32[]{:S(2)}, u32[]{:S(2)}) %collective-permute-start) | collective-permute-done | bytes 262176 | tf_op jit(solution)/shard_map/ppermute | solution.py:195
  24.0 2.7 %basis.1 = (f32[512,128]{1,0:T(8,128)S(1)}, f32[256,512]{1,0:T(8,128)S(1)}) custom-call(s32[7,4]{1,0:T(8,128)S(1)} %copy.6.cols_ref, f32[256,256]{1,0:T(8,128)S(1)} %pack.1.own_ref, f32[256,256]{1,0:T(8,128)S(1)} %collective-permute-done.pair_ref, f32[256,256]{1,0:T(8,128)S(1)} %collective-permute-done.1.other_ref), custom_call_target="tpu_custom_call" | custom-call | tf_op jit(solution)/shard_map/basis/pallas_call | solution.py:176
  26.7 12.6 %all_to_all.15.in_ref = f32[32,16,128]{2,1,0:T(8,128)S(1)} all-to-all(f32[32,16,128]{2,1,0:T(8,128)S(1)} %bitcast.3), channel_id=1, replica_groups=mesh['y'=4,'z'=16,'x'=4,'core'=2] {'y','x','core'}, dimensions={0} | all-to-all | bytes 524288 | tf_op jit(solution)/shard_map/all_to_all | solution.py:198
  39.4 20.4 %all_to_all.16.in_ref = f32[16,16,128]{2,1,0:T(8,128)S(1)} all-to-all(f32[16,16,128]{2,1,0:T(8,128)S(1)} %total.2), channel_id=1, replica_groups=mesh['y'=4,'z'=16,'x'=4,'core'=2] {'z'}, dimensions={0} | all-to-all | bytes 262144 | tf_op jit(solution)/shard_map/all_to_all | solution.py:199
  59.8 0.0 copy-start.2
  59.8 15.3 %all_to_all.17 = f32[32,16,128]{2,1,0:T(8,128)S(1)} all-to-all(f32[32,16,128]{2,1,0:T(8,128)S(1)} %total.3), channel_id=1, replica_groups=mesh['y'=4,'z'=16,'x'=4,'core'=2] {'y','x','core'}, dimensions={0} | all-to-all | bytes 524288 | tf_op jit(solution)/shard_map/all_to_all | solution.py:200
  75.1 0.0 copy-done.2
  75.1 25.1 %solve.1 = (f32[64,256]{1,0:T(8,128)}, f32[64,256]{1,0:T(8,128)}) custom-call(f32[512,128]{1,0:T(8,128)S(1)} %bitcast.2, f32[256,512]{1,0:T(8,128)S(1)} %get-tuple-element.5.stack_ref, f32[64,256]{1,0:T(8,128)S(1)} %copy-done.2), custom_call_target="tpu_custom_call" | custom-call | tf_op jit(solution)/shard_map/solve/pallas_call | solution.py:185
  (2 shorter events, 0.1 us)
Async XLA Ops:
  1.4 1.0 %copy-start = (f32[7,64,256]{2,1,0:T(8,128)S(1)}, f32[7,64,256]{2,1,0:T(8,128)}, u32[]{:S(2)}) copy-start(f32[7,64,256]{2,1,0:T(8,128)} %blocks_ref.1) | copy-start | bytes 1376260
  2.4 0.8 copy-start.1
  3.9 18.9 %collective-permute-start.1 = (f32[256,256]{1,0:T(8,128)S(1)}, f32[256,256]{1,0:T(8,128)S(1)}, u32[]{:S(2)}, u32[]{:S(2)}) collective-permute-start(f32[256,256]{1,0:T(8,128)S(1)} %pack.1.own_ref), channel_id=1, source_target_pairs={{0,511},{1,2},{2,1},{3,4},{4,3},{5,6},{6,5},{7,8},{8,7},{9,10},{10... | collective-permute-start | bytes 786440 | tf_op jit(solution)/shard_map/ppermute | solution.py:196
  8.4 15.5 %collective-permute-start = (f32[256,256]{1,0:T(8,128)S(1)}, f32[256,256]{1,0:T(8,128)S(1)}, u32[]{:S(2)}, u32[]{:S(2)}) collective-permute-start(f32[256,256]{1,0:T(8,128)S(1)} %pack.1.own_ref), channel_id=1, source_target_pairs={{0,1},{1,0},{2,3},{3,2},{4,5},{5,4},{6,7},{7,6},{8,9},{9,8},{10,11... | collective-permute-start | bytes 786440 | tf_op jit(solution)/shard_map/ppermute | solution.py:195
  59.8 15.3 %copy-start.2 = (f32[64,256]{1,0:T(8,128)S(1)}, f32[64,256]{1,0:T(8,128)}, u32[]{:S(2)}) copy-start(f32[64,256]{1,0:T(8,128)} %right_ref.3) | copy-start | bytes 196612

commit v2 on v1

v2 whole, which is shorter than its diff:
```python
import functools

import jax
import jax.numpy as jnp
from jax import lax
from jax.experimental import pallas as pl
from jax.experimental.pallas import tpu as pltpu
from jax.sharding import Mesh, PartitionSpec as P

SCALE = 1.25
S = 4
BS = 64
HIGH = lax.Precision.HIGHEST

HBM = pl.BlockSpec(memory_space=pltpu.HBM)
VMEM = pl.BlockSpec(memory_space=pltpu.VMEM)
SMEM = pl.BlockSpec(memory_space=pltpu.SMEM)


def dot(a, b, dims):
    return lax.dot_general(a, b, (dims, ((), ())), precision=HIGH, preferred_element_type=jnp.float32)


def pack_kernel(total_blocks, cols_ref, right_ref, blocks_ref, out_ref, part_ref, part_sem, right_sem):
    slots, _, width = part_ref.shape
    copies = [pltpu.make_async_copy(blocks_ref.at[slot], part_ref.at[slot], part_sem.at[slot]) for slot in range(slots)]
    for copy in copies:
        copy.start()
    last = pltpu.make_async_copy(right_ref, out_ref.at[192:256], right_sem)
    last.start()
    lane = lax.broadcasted_iota(jnp.int32, (1, width), 1) // BS
    offsets = []
    for slot in (5, 6):
        offset = jnp.zeros((1, width), jnp.int32)
        for row in range(width // BS):
            delta = cols_ref[row, slot] - cols_ref[row, 0]
            delta = jnp.where(delta > 1, delta - total_blocks, delta)
            delta = jnp.where(delta < -1, delta + total_blocks, delta)
            offset = jnp.where(lane == row, delta, offset)
        offsets.append(offset)
    for copy in copies:
        copy.wait()
    for at, value, fixed in ((0, -1, (2, 4)), (64, 0, (0,)), (128, 1, (1, 3))):
        kept = sum(part_ref[slot] for slot in fixed)
        for slot, offset in zip((5, 6), offsets):
            kept = kept + jnp.where(offset == value, part_ref[slot], 0.0)
        out_ref[at : at + 64, :] = kept
    last.wait()


def basis_kernel(cols_ref, own_ref, pair_ref, other_ref, sums_ref, stack_ref, ext_ref, band_ref):
    even = lax.rem(cols_ref[0, 0] // 4, 2) == 0

    @pl.when(even)
    def _():
        ext_ref[:, 0:256] = other_ref[...]
        ext_ref[:, 512:768] = pair_ref[...]

    @pl.when(jnp.logical_not(even))
    def _():
        ext_ref[:, 0:256] = pair_ref[...]
        ext_ref[:, 512:768] = other_ref[...]

    ext_ref[:, 256:512] = own_ref[...]
    left = lax.broadcasted_iota(jnp.int32, (BS, 128), 1) < BS
    for p in range(6):
        at = slice(128 * p, 128 * (p + 1))
        minus, zero, plus = ext_ref[0:64, at], ext_ref[64:128, at], ext_ref[128:192, at]
        band_ref[p, 0:64, :] = jnp.where(left, minus, 0.0)
        band_ref[p, 64:128, :] = jnp.where(left, zero, minus)
        band_ref[p, 128:192, :] = jnp.where(left, plus, zero)
        band_ref[p, 192:256, :] = jnp.where(left, 0.0, plus)
    current = ext_ref[192:256, :]
    first = 0
    own = [current[:, 256:512]]
    images = []
    for step, (low, high) in enumerate(((0, 6), (1, 5), (1, 5), (2, 4))):
        rolled = pltpu.roll(current, 64, 1)
        parts = []
        for p in range(low, high):
            at = 128 * (p - first)
            if at + 256 <= rolled.shape[1]:
                window = rolled[:, at : at + 256]
            else:
                window = jnp.concatenate([rolled[:, at:], rolled[:, :128]], axis=1)
            parts.append(dot(window, band_ref[p], ((1,), (0,))))
        product = jnp.concatenate(parts, axis=1)
        inner = product[:, 256 - 128 * low : 512 - 128 * low]
        images.append(own[step] + inner)
        current = SCALE * product
        first = low
        own.append(SCALE * inner)
    w = jnp.concatenate(images, axis=0)
    stack_ref[:, 0:256] = jnp.concatenate(own[:S], axis=0)
    stack_ref[:, 256:512] = w
    z = jnp.concatenate([w, own[0]], axis=0)
    g = [dot(images[k], z[64 * k :], ((1,), (1,))) for k in range(S)]
    sums_ref[0:64, :] = g[0][:, 0:128]
    sums_ref[64:128, :] = g[0][:, 128:256]
    sums_ref[128:192, :] = g[1][:, 0:128]
    sums_ref[192:256, :] = g[1][:, 128:256]
    sums_ref[256:320, :] = g[2][:, 0:128]
    sums_ref[320:384, :] = g[3]
    sums_ref[384:448, :] = jnp.concatenate([g[0][:, 256:320], g[2][:, 128:192]], axis=1)
    sums_ref[448:512, :] = jnp.zeros((64, 128), jnp.float32)


def total_kernel(copies, in_ref, out_ref):
    total = in_ref[0]
    for k in range(1, in_ref.shape[0]):
        total = total + in_ref[k]
    for k in range(copies):
        out_ref[k] = total


WINDOW = 3


def inverse_of(x):
    return 1.0 / x


def eliminate(part):
    groups, tiles = BS // 8, len(part[0])
    rows = lax.broadcasted_iota(jnp.int32, (8, 1), 0)
    scaled = [[None] * tiles for _ in range(groups)]

    def fetch(k, begin):
        return {g: jnp.broadcast_to(part[g][0][:, k : k + 1], (8, 128)) for g in range(begin, groups)}

    ahead = {k: fetch(k, 0) for k in range(2 * WINDOW)}
    for k in range(0, BS, 2):
        at, row = k // 8, k % 8
        first, second = ahead.pop(k), ahead.pop(k + 1)
        a, b, d = first[at][row : row + 1, :], first[at][row + 1 : row + 2, :], second[at][row + 1 : row + 2, :]
        inverse = inverse_of(a * d - b * b)
        p, q, r = d * inverse, -b * inverse, a * inverse

        def solved(top, low):
            n = top.shape[1]
            return p[:, :n] * top + q[:, :n] * low, q[:, :n] * top + r[:, :n] * low

        if row < 6:
            keep = rows > row + 1
            first[at], second[at] = jnp.where(keep, first[at], 0.0), jnp.where(keep, second[at], 0.0)
            live = range(at, groups)
        else:
            live = range(at + 1, groups)
        for column in ahead.values():
            top, low = solved(column[at][row : row + 1, :], column[at][row + 1 : row + 2, :])
            for g in live:
                if g in column:
                    column[g] = column[g] - (first[g] * top + second[g] * low)
        for t in range(tiles):
            top, low = solved(part[at][t][row : row + 1, :], part[at][t][row + 1 : row + 2, :])
            n = top.shape[1]
            for g in live:
                part[g][t] = part[g][t] - (first[g][:, :n] * top + second[g][:, :n] * low)
            pair = jnp.where(rows == row, top, low)
            scaled[at][t] = pair if row == 0 else jnp.where(rows < row, scaled[at][t], pair)
        for late in (k + 2 * WINDOW, k + 2 * WINDOW + 1):
            if late < BS:
                ahead[late] = fetch(late, (k + 2) // 8)
    join = lambda x: [jnp.concatenate([x[g][t] for g in range(groups)], axis=0) for t in range(tiles)]
    return join(part), join(scaled)


def solve_kernel(sums_ref, stack_ref, update_ref, residual_ref):
    u = [sums_ref[64 * k : 64 * (k + 1), :] for k in range(7)]
    row = lax.broadcasted_iota(jnp.int32, (BS, 128), 0)
    lane = lax.broadcasted_iota(jnp.int32, (BS, 128), 1)
    eye = jnp.where(row == lane % BS, 1.0, 0.0)
    left = lane < BS
    half = lambda tiles, i: tiles[i // 2][:, 64 * (i % 2) : 64 * (i % 2 + 1)]
    tiles = {
        0: [u[0], u[1], jnp.where(left, u[6], eye)],
        1: [u[2], u[3], eye[:, 0:64]],
        2: [u[4], jnp.where(left, eye, u[6])],
        3: [u[5], eye[:, 0:64]],
    }
    order = {0: (0, 1, 2, 3, 4, 5), 1: (1, 2, 3, 4, 5), 2: (2, 3, 5, 4), 3: (3, 4, 5)}
    solved = {}
    for k in range(S):
        part = [[t[8 * g : 8 * (g + 1), :] for t in tiles[k]] for g in range(BS // 8)]
        part, scaled = eliminate(part)
        y = {name: half(part, i) for i, name in enumerate(order[k])}
        z = {name: half(scaled, i) for i, name in enumerate(order[k])}
        for i in range(k + 1, S):
            names = [n for n in order[i] if n < 5]
            change = dot(y[i], jnp.concatenate([z[n] for n in names], axis=1), ((0,), (0,)))
            fresh = []
            for t, tile in enumerate(tiles[i]):
                have = order[i][2 * t : 2 * t + 2]
                cut = [change[:, 64 * names.index(n) : 64 * (names.index(n) + 1)] if n < 5 else jnp.zeros((BS, BS), jnp.float32) for n in have]
                whole = all(n < 5 for n in have)
                if whole:
                    fresh.append(tile - change[:, 64 * names.index(have[0]) : 64 * names.index(have[0]) + 64 * len(have)])
                elif any(n < 5 for n in have):
                    fresh.append(tile - jnp.concatenate(cut, axis=1))
                else:
                    fresh.append(tile)
            tiles[i] = fresh
        names = [n for n in range(k + 1, 5)]
        solved[k] = dot(y[5], jnp.concatenate([z[n] for n in names], axis=1), ((0,), (0,)))
    x = [None] * S
    both = None
    for k in range(S - 1, -1, -1):
        x[k] = solved[k][:, 64 * (S - 1 - k) : 64 * (S - k)]
        if k < S - 1:
            x[k] = x[k] - dot(solved[k][:, : 64 * (S - 1 - k)], jnp.concatenate(x[k + 1 :], axis=0), ((1,), (0,)))
        term = dot(x[k], stack_ref[64 * k : 64 * (k + 1), :], ((0,), (0,)))
        both = term if both is None else both + term
    update_ref[...] = both[:, 0:256]
    residual_ref[...] = stack_ref[0:64, 0:256] - both[:, 256:512]


def call(kernel, outs, in_specs, scratch=(), name=None):
    shapes = [jax.ShapeDtypeStruct(s, jnp.float32) for s in outs]
    specs = [VMEM] * len(outs)
    return pl.pallas_call(
        kernel,
        out_shape=shapes if len(outs) > 1 else shapes[0],
        in_specs=in_specs,
        out_specs=specs if len(outs) > 1 else specs[0],
        scratch_shapes=list(scratch),
        name=name,
        compiler_params=pltpu.CompilerParams(vmem_limit_bytes=48 * 1024 * 1024),
    )


def pack(cols, right_side, blocks, total_blocks):
    kernel = functools.partial(pack_kernel, total_blocks)
    scratch = (pltpu.VMEM(blocks.shape, jnp.float32), pltpu.SemaphoreType.DMA((blocks.shape[0],)), pltpu.SemaphoreType.DMA)
    return call(kernel, [(256, 256)], [SMEM, HBM, HBM], scratch, name="pack")(cols, *(pltpu.with_memory_space_constraint(a, pltpu.HBM) for a in (right_side, blocks)))


def basis(cols, own, pair, other):
    scratch = (pltpu.VMEM((256, 768), jnp.float32), pltpu.VMEM((6, 256, 128), jnp.float32))
    return call(basis_kernel, [(512, 128), (256, 512)], [SMEM, VMEM, VMEM, VMEM], scratch, name="basis")(cols, own, pair, other)


def total(parts, copies):
    kernel = functools.partial(total_kernel, copies)
    return call(kernel, [(copies,) + parts.shape[1:]], [VMEM], name="total")(parts)


def solve(sums, stack):
    return call(solve_kernel, [(64, 256), (64, 256)], [VMEM, VMEM], name="solve")(sums, stack)


AXES = ("y", "z", "x", "core")
PLANE = ("y", "x", "core")


def shards(right_side, blocks, cols):
    devices = lax.axis_size(AXES)
    cols = cols.T
    own = pack(cols, right_side, blocks, cols.shape[0] * devices)
    pair = lax.ppermute(own, AXES, [(i, i ^ 1) for i in range(devices)])
    other = lax.ppermute(own, AXES, [(i, ((i - 1) ^ 1) + 1 if i else devices - 1) if i < devices - 1 else (i, 0) for i in range(devices)])
    sums, stack = basis(cols, own, pair, other)
    parts = lax.all_to_all(sums.reshape(32, 16, 128), PLANE, 0, 0)
    parts = lax.all_to_all(total(parts, 16), "z", 0, 0)
    sums = lax.all_to_all(total(parts, 32), PLANE, 0, 0)
    return tuple(solve(sums.reshape(512, 128), stack))


def solution(mesh):
    grid = Mesh(mesh.devices.reshape(4, 16, 4, 2), AXES)
    in_specs = (P(None, AXES), P(None, None, AXES), P(None, AXES))
    out_specs = (P(None, AXES), P(None, AXES))
    return jax.shard_map(shards, mesh=grid, in_specs=in_specs, out_specs=out_specs, check_vma=False)
```

time: 101 us -> 83.6 us (0.83)
  Pallas kernels: 28.6 us -> 13.7 us
  local copies, waits for them, and re-layouts: 2.63 us -> 0.67 us
    pallas_call x2, Pallas kernels: 25.8 us -> 10.7 us  [the longest x1 8.98 us: solve(): call(solve_kernel, [(64, 256), (64, 256)], [VMEM, VMEM], name='solve')]
    unnamed x7 -> x2, local copies, waits for them, and re-layouts: 2.63 us -> 0.67 us
where the time goes in v2:
time: 83.6 us; the launch traced here: 83.2 us
  blocking collectives  48.1 us (58%)
  starting transfers between devices  18.9 us (23%)
  Pallas kernels  13.7 us (16%)
  waiting for transfers between devices  1.13 us (1%)
    all_to_all x1, blocking collectives, shards(): parts = lax.all_to_all(total(parts, 16), 'z', 0, 0)  20.4 us
    all_to_all x1, blocking collectives, shards(): sums = lax.all_to_all(total(parts, 32), PLANE, 0, 0)  15.1 us
    ppermute x1, starting transfers between devices, shards(): pair = lax.ppermute(own, AXES, [(i, i ^ 1) for i in range(devices)])  14.4 us
    all_to_all x1, blocking collectives, shards(): parts = lax.all_to_all(sums.reshape(32, 16, 128), PLANE, 0, 0)  12.6 us
    pallas_call x1, Pallas kernels, solve(): call(solve_kernel, [(64, 256), (64, 256)], [VMEM, VMEM], name='solve')  8.98 us
    ppermute x1, starting transfers between devices, shards(): lax.ppermute(own, AXES, [(i, (i - 1 ^ 1) + 1 if i else devices - 1) if i...  4.5 us
    pallas_call x1, Pallas kernels, basis(): call(basis_kernel, [(512, 128), (256, 512)], [SMEM, VMEM, VMEM, VMEM], sc...  2.96 us
    pallas_call x1, Pallas kernels, pack(): call(kernel, [(256, 256)], [SMEM, HBM, HBM], scratch, name='pack')  1.7 us
  transfers between devices with their start and end apart: 2, of which 1 were waited for; matrix products, arithmetic and copies ran while one was open for 0% of the time, Pallas kernels for 0%

profile of v2, /device:TPU:1, one launch (start us, length us, event | category | flops | bytes accessed | tf_op | source)
XLA Modules:
  0.0 83.2 jit_solution(6567893949303512957)
XLA Ops:
  0.6 0.0 copy-start
  0.6 0.7 copy-done
  1.3 1.7 %pack.1.own_ref = f32[256,256]{1,0:T(8,128)S(1)} custom-call(s32[4,7]{1,0:T(4,128)S(1)} %bitcast.5, f32[64,256]{1,0:T(8,128)} %right_ref.1, f32[7,64,256]{2,1,0:T(8,128)} %blocks_ref.1), custom_call_target="tpu_custom_call" | custom-call | tf_op jit(solution)/shard_map/pack/pallas_call | solution.py:234
  3.0 4.5 %collective-permute-start.1 = (f32[256,256]{1,0:T(8,128)S(1)}, f32[256,256]{1,0:T(8,128)S(1)}, u32[]{:S(2)}, u32[]{:S(2)}) collective-permute-start(f32[256,256]{1,0:T(8,128)S(1)} %pack.1.own_ref), channel_id=1, source_target_pairs={{0,511},{1,2},{2,1},{3,4},{4,3},{5,6},{6,5},{7,8},{8,7},{9,10},{10... | collective-permute-start | bytes 786440 | tf_op jit(solution)/shard_map/ppermute | solution.py:260
  7.5 14.4 %collective-permute-start = (f32[256,256]{1,0:T(8,128)S(1)}, f32[256,256]{1,0:T(8,128)S(1)}, u32[]{:S(2)}, u32[]{:S(2)}) collective-permute-start(f32[256,256]{1,0:T(8,128)S(1)} %pack.1.own_ref), channel_id=1, source_target_pairs={{0,1},{1,0},{2,3},{3,2},{4,5},{5,4},{6,7},{7,6},{8,9},{9,8},{10,11... | collective-permute-start | bytes 786440 | tf_op jit(solution)/shard_map/ppermute | solution.py:259
  21.9 0.0 collective-permute-done.1.other_ref
  21.9 1.1 %collective-permute-done.pair_ref = f32[256,256]{1,0:T(8,128)S(1)} collective-permute-done((f32[256,256]{1,0:T(8,128)S(1)}, f32[256,256]{1,0:T(8,128)S(1)}, u32[]{:S(2)}, u32[]{:S(2)}) %collective-permute-start) | collective-permute-done | bytes 262176 | tf_op jit(solution)/shard_map/ppermute | solution.py:259
  23.1 3.0 %basis.1 = (f32[512,128]{1,0:T(8,128)S(1)}, f32[256,512]{1,0:T(8,128)S(1)}) custom-call(s32[4,7]{1,0:T(4,128)S(1)} %bitcast.6, f32[256,256]{1,0:T(8,128)S(1)} %pack.1.own_ref, f32[256,256]{1,0:T(8,128)S(1)} %collective-permute-done.pair_ref, f32[256,256]{1,0:T(8,128)S(1)} %collective-permute-done.1.other_ref), custom_call_target="tpu_custom_call" | custom-call | tf_op jit(solution)/shard_map/basis/pallas_call | solution.py:239
  26.0 12.6 %all_to_all.15.in_ref = f32[32,16,128]{2,1,0:T(8,128)S(1)} all-to-all(f32[32,16,128]{2,1,0:T(8,128)S(1)} %bitcast.4), channel_id=1, replica_groups=mesh['y'=4,'z'=16,'x'=4,'core'=2] {'y','x','core'}, dimensions={0} | all-to-all | bytes 524288 | tf_op jit(solution)/shard_map/all_to_all | solution.py:262
  38.7 20.4 %all_to_all.16.in_ref = f32[16,16,128]{2,1,0:T(8,128)S(1)} all-to-all(f32[16,16,128]{2,1,0:T(8,128)S(1)} %total.2), channel_id=1, replica_groups=mesh['y'=4,'z'=16,'x'=4,'core'=2] {'z'}, dimensions={0} | all-to-all | bytes 262144 | tf_op jit(solution)/shard_map/all_to_all | solution.py:263
  59.1 15.1 %all_to_all.17 = f32[32,16,128]{2,1,0:T(8,128)S(1)} all-to-all(f32[32,16,128]{2,1,0:T(8,128)S(1)} %total.3), channel_id=1, replica_groups=mesh['y'=4,'z'=16,'x'=4,'core'=2] {'y','x','core'}, dimensions={0} | all-to-all | bytes 524288 | tf_op jit(solution)/shard_map/all_to_all | solution.py:264
  74.2 9.0 %solve.1 = (f32[64,256]{1,0:T(8,128)}, f32[64,256]{1,0:T(8,128)}) custom-call(f32[512,128]{1,0:T(8,128)S(1)} %bitcast.3, f32[256,512]{1,0:T(8,128)S(1)} %get-tuple-element.5.stack_ref), custom_call_target="tpu_custom_call" | custom-call | tf_op jit(solution)/shard_map/solve/pallas_call | solution.py:248
  (2 shorter events, 0.1 us)
Async XLA Ops:
  0.6 0.7 copy-start
  3.0 18.9 %collective-permute-start.1 = (f32[256,256]{1,0:T(8,128)S(1)}, f32[256,256]{1,0:T(8,128)S(1)}, u32[]{:S(2)}, u32[]{:S(2)}) collective-permute-start(f32[256,256]{1,0:T(8,128)S(1)} %pack.1.own_ref), channel_id=1, source_target_pairs={{0,511},{1,2},{2,1},{3,4},{4,3},{5,6},{6,5},{7,8},{8,7},{9,10},{10... | collective-permute-start | bytes 786440 | tf_op jit(solution)/shard_map/ppermute | solution.py:260
  7.5 15.5 %collective-permute-start = (f32[256,256]{1,0:T(8,128)S(1)}, f32[256,256]{1,0:T(8,128)S(1)}, u32[]{:S(2)}, u32[]{:S(2)}) collective-permute-start(f32[256,256]{1,0:T(8,128)S(1)} %pack.1.own_ref), channel_id=1, source_target_pairs={{0,1},{1,0},{2,3},{3,2},{4,5},{5,4},{6,7},{7,6},{8,9},{9,8},{10,11... | collective-permute-start | bytes 786440 | tf_op jit(solution)/shard_map/ppermute | solution.py:259

commit v3 on v2

--- a/solution.py
+++ b/solution.py
@@ -10,25 +10,25 @@
 SCALE = 1.25
 S = 4
 BS = 64
-HIGH = lax.Precision.HIGHEST
 
 HBM = pl.BlockSpec(memory_space=pltpu.HBM)
 VMEM = pl.BlockSpec(memory_space=pltpu.VMEM)
 SMEM = pl.BlockSpec(memory_space=pltpu.SMEM)
 
 
-def dot(a, b, dims):
-    return lax.dot_general(a, b, (dims, ((), ())), precision=HIGH, preferred_element_type=jnp.float32)
-
-
-def pack_kernel(total_blocks, cols_ref, right_ref, blocks_ref, out_ref, part_ref, part_sem, right_sem):
+def pack_kernel(total_blocks, cols_hbm, right_ref, blocks_ref, out_ref, flag_ref, cols_ref, part_ref, cols_sem, part_sem, right_sem):
     slots, _, width = part_ref.shape
+    table = pltpu.make_async_copy(cols_hbm, cols_ref, cols_sem)
+    table.start()
     copies = [pltpu.make_async_copy(blocks_ref.at[slot], part_ref.at[slot], part_sem.at[slot]) for slot in range(slots)]
     for copy in copies:
         copy.start()
     last = pltpu.make_async_copy(right_ref, out_ref.at[192:256], right_sem)
     last.start()
     lane = lax.broadcasted_iota(jnp.int32, (1, width), 1) // BS
+    table.wait()
+    odd = lax.rem(cols_ref[0, 0] // (width // BS), 2)
+    flag_ref[...] = jnp.full(flag_ref.shape, 1 - odd, jnp.int32).astype(jnp.float32)
     offsets = []
     for slot in (5, 6):
         offset = jnp.zeros((1, width), jnp.int32)
@@ -48,53 +48,63 @@
     last.wait()
 
 
-def basis_kernel(cols_ref, own_ref, pair_ref, other_ref, sums_ref, stack_ref, ext_ref, band_ref):
-    even = lax.rem(cols_ref[0, 0] // 4, 2) == 0
-
-    @pl.when(even)
-    def _():
-        ext_ref[:, 0:256] = other_ref[...]
-        ext_ref[:, 512:768] = pair_ref[...]
-
-    @pl.when(jnp.logical_not(even))
-    def _():
-        ext_ref[:, 0:256] = pair_ref[...]
-        ext_ref[:, 512:768] = other_ref[...]
-
-    ext_ref[:, 256:512] = own_ref[...]
+def halves(a):
+    high = a.astype(jnp.bfloat16)
+    return high, (a - high.astype(jnp.float32)).astype(jnp.bfloat16)
+
+
+def product(a, b, dims):
+    one = lambda x, y: lax.dot_general(x, y, (dims, ((), ())), preferred_element_type=jnp.float32)
+    return one(a[0], b[0]) + (one(a[0], b[1]) + one(a[1], b[0]))
+
+
+def basis_kernel(flag_ref, own_ref, pair_ref, other_ref, sums_ref, stack_ref):
+    even = flag_ref[0:1, :] > 0
     left = lax.broadcasted_iota(jnp.int32, (BS, 128), 1) < BS
+    bands, tiles = [], []
     for p in range(6):
-        at = slice(128 * p, 128 * (p + 1))
-        minus, zero, plus = ext_ref[0:64, at], ext_ref[64:128, at], ext_ref[128:192, at]
-        band_ref[p, 0:64, :] = jnp.where(left, minus, 0.0)
-        band_ref[p, 64:128, :] = jnp.where(left, zero, minus)
-        band_ref[p, 128:192, :] = jnp.where(left, plus, zero)
-        band_ref[p, 192:256, :] = jnp.where(left, 0.0, plus)
-    current = ext_ref[192:256, :]
+        at = slice(128 * (p % 2), 128 * (p % 2 + 1))
+        if p < 2:
+            get = lambda r: jnp.where(even, other_ref[r, at], pair_ref[r, at])
+        elif p < 4:
+            get = lambda r: own_ref[r, at]
+        else:
+            get = lambda r: jnp.where(even, pair_ref[r, at], other_ref[r, at])
+        minus, zero, plus = get(slice(0, 64)), get(slice(64, 128)), get(slice(128, 192))
+        band = jnp.concatenate(
+            [
+                jnp.where(left, minus, 0.0),
+                jnp.where(left, zero, minus),
+                jnp.where(left, plus, zero),
+                jnp.where(left, 0.0, plus),
+            ],
+            axis=0,
+        )
+        bands.append(halves(SCALE * band))
+        tiles.append(get(slice(192, 256)))
+    own = [jnp.concatenate(tiles[2:4], axis=1)]
     first = 0
-    own = [current[:, 256:512]]
-    images = []
-    for step, (low, high) in enumerate(((0, 6), (1, 5), (1, 5), (2, 4))):
-        rolled = pltpu.roll(current, 64, 1)
-        parts = []
+    for low, high in ((0, 6), (1, 5), (1, 5), (2, 4)):
+        current = jnp.concatenate(tiles, axis=1)
+        rolled = halves(pltpu.roll(current, 64, 1))
+        fresh = []
         for p in range(low, high):
             at = 128 * (p - first)
-            if at + 256 <= rolled.shape[1]:
-                window = rolled[:, at : at + 256]
+            if at + 256 <= current.shape[1]:
+                window = [r[:, at : at + 256] for r in rolled]
             else:
-                window = jnp.concatenate([rolled[:, at:], rolled[:, :128]], axis=1)
-            parts.append(dot(window, band_ref[p], ((1,), (0,))))
-        product = jnp.concatenate(parts, axis=1)
-        inner = product[:, 256 - 128 * low : 512 - 128 * low]
-        images.append(own[step] + inner)
-        current = SCALE * product
+                window = [jnp.concatenate([r[:, at:], r[:, :128]], axis=1) for r in rolled]
+            fresh.append(product(window, bands[p], ((1,), (0,))))
+        own.append(jnp.concatenate(fresh[2 - low : 4 - low], axis=1))
+        tiles = fresh
         first = low
-        own.append(SCALE * inner)
+    images = [own[k] + own[k + 1] / SCALE for k in range(S)]
     w = jnp.concatenate(images, axis=0)
     stack_ref[:, 0:256] = jnp.concatenate(own[:S], axis=0)
     stack_ref[:, 256:512] = w
     z = jnp.concatenate([w, own[0]], axis=0)
-    g = [dot(images[k], z[64 * k :], ((1,), (1,))) for k in range(S)]
+    z = halves(z)
+    g = [product([h[64 * k : 64 * (k + 1)] for h in z], [h[64 * k :] for h in z], ((1,), (1,))) for k in range(S)]
     sums_ref[0:64, :] = g[0][:, 0:128]
     sums_ref[64:128, :] = g[0][:, 128:256]
     sums_ref[128:192, :] = g[1][:, 0:128]
@@ -113,11 +123,11 @@
         out_ref[k] = total
 
 
-WINDOW = 3
-
-
-def inverse_of(x):
-    return 1.0 / x
+WINDOW = 4
+
+
+def narrow(a, b, dims):
+    return product(halves(a), halves(b), dims)
 
 
 def eliminate(part):
@@ -133,7 +143,7 @@
         at, row = k // 8, k % 8
         first, second = ahead.pop(k), ahead.pop(k + 1)
         a, b, d = first[at][row : row + 1, :], first[at][row + 1 : row + 2, :], second[at][row + 1 : row + 2, :]
-        inverse = inverse_of(a * d - b * b)
+        inverse = 1.0 / (a * d - b * b)
         p, q, r = d * inverse, -b * inverse, a * inverse
 
         def solved(top, low):
@@ -179,7 +189,8 @@
         3: [u[5], eye[:, 0:64]],
     }
     order = {0: (0, 1, 2, 3, 4, 5), 1: (1, 2, 3, 4, 5), 2: (2, 3, 5, 4), 3: (3, 4, 5)}
-    solved = {}
+    spans = [stack_ref[64 * k : 64 * (k + 1), :] for k in range(S)]
+    both = None
     for k in range(S):
         part = [[t[8 * g : 8 * (g + 1), :] for t in tiles[k]] for g in range(BS // 8)]
         part, scaled = eliminate(part)
@@ -187,29 +198,24 @@
         z = {name: half(scaled, i) for i, name in enumerate(order[k])}
         for i in range(k + 1, S):
             names = [n for n in order[i] if n < 5]
-            change = dot(y[i], jnp.concatenate([z[n] for n in names], axis=1), ((0,), (0,)))
+            change = narrow(y[i], jnp.concatenate([z[n] for n in names], axis=1), ((0,), (0,)))
             fresh = []
             for t, tile in enumerate(tiles[i]):
                 have = order[i][2 * t : 2 * t + 2]
                 cut = [change[:, 64 * names.index(n) : 64 * (names.index(n) + 1)] if n < 5 else jnp.zeros((BS, BS), jnp.float32) for n in have]
-                whole = all(n < 5 for n in have)
-                if whole:
-                    fresh.append(tile - change[:, 64 * names.index(have[0]) : 64 * names.index(have[0]) + 64 * len(have)])
+                if all(n < 5 for n in have):
+                    at = 64 * names.index(have[0])
+                    fresh.append(tile - change[:, at : at + 64 * len(have)])
                 elif any(n < 5 for n in have):
                     fresh.append(tile - jnp.concatenate(cut, axis=1))
                 else:
                     fresh.append(tile)
             tiles[i] = fresh
-        names = [n for n in range(k + 1, 5)]
-        solved[k] = dot(y[5], jnp.concatenate([z[n] for n in names], axis=1), ((0,), (0,)))
-    x = [None] * S
-    both = None
-    for k in range(S - 1, -1, -1):
-        x[k] = solved[k][:, 64 * (S - 1 - k) : 64 * (S - k)]
-        if k < S - 1:
-            x[k] = x[k] - dot(solved[k][:, : 64 * (S - 1 - k)], jnp.concatenate(x[k + 1 :], axis=0), ((1,), (0,)))
-        term = dot(x[k], stack_ref[64 * k : 64 * (k + 1), :], ((0,), (0,)))
+        solved = narrow(y[5], jnp.concatenate([z[n] for n in range(k + 1, 5)], axis=1), ((0,), (0,)))
+        term = narrow(solved[:, 64 * (S - 1 - k) :], spans[k], ((0,), (0,)))
         both = term if both is None else both + term
+        for i in range(k + 1, S):
+            spans[i] = spans[i] - narrow(solved[:, 64 * (i - k - 1) : 64 * (i - k)], spans[k], ((0,), (0,)))
     update_ref[...] = both[:, 0:256]
     residual_ref[...] = stack_ref[0:64, 0:256] - both[:, 256:512]
 
@@ -230,13 +236,19 @@
 
 def pack(cols, right_side, blocks, total_blocks):
     kernel = functools.partial(pack_kernel, total_blocks)
-    scratch = (pltpu.VMEM(blocks.shape, jnp.float32), pltpu.SemaphoreType.DMA((blocks.shape[0],)), pltpu.SemaphoreType.DMA)
-    return call(kernel, [(256, 256)], [SMEM, HBM, HBM], scratch, name="pack")(cols, *(pltpu.with_memory_space_constraint(a, pltpu.HBM) for a in (right_side, blocks)))
-
-
-def basis(cols, own, pair, other):
-    scratch = (pltpu.VMEM((256, 768), jnp.float32), pltpu.VMEM((6, 256, 128), jnp.float32))
-    return call(basis_kernel, [(512, 128), (256, 512)], [SMEM, VMEM, VMEM, VMEM], scratch, name="basis")(cols, own, pair, other)
+    scratch = (
+        pltpu.SMEM(cols.shape, jnp.int32),
+        pltpu.VMEM(blocks.shape, jnp.float32),
+        pltpu.SemaphoreType.DMA,
+        pltpu.SemaphoreType.DMA((blocks.shape[0],)),
+        pltpu.SemaphoreType.DMA,
+    )
+    arrays = [pltpu.with_memory_space_constraint(a, pltpu.HBM) for a in (cols, right_side, blocks)]
+    return call(kernel, [(256, 256), (8, 128)], [HBM] * 3, scratch, name="pack")(*arrays)
+
+
+def basis(flag, own, pair, other):
+    return call(basis_kernel, [(512, 128), (256, 512)], [VMEM] * 4, name="basis")(flag, own, pair, other)
 
 
 def total(parts, copies):
@@ -255,10 +267,10 @@
 def shards(right_side, blocks, cols):
     devices = lax.axis_size(AXES)
     cols = cols.T
-    own = pack(cols, right_side, blocks, cols.shape[0] * devices)
+    own, flag = pack(cols, right_side, blocks, cols.shape[0] * devices)
     pair = lax.ppermute(own, AXES, [(i, i ^ 1) for i in range(devices)])
     other = lax.ppermute(own, AXES, [(i, ((i - 1) ^ 1) + 1 if i else devices - 1) if i < devices - 1 else (i, 0) for i in range(devices)])
-    sums, stack = basis(cols, own, pair, other)
+    sums, stack = basis(flag, own, pair, other)
     parts = lax.all_to_all(sums.reshape(32, 16, 128), PLANE, 0, 0)
     parts = lax.all_to_all(total(parts, 16), "z", 0, 0)
     sums = lax.all_to_all(total(parts, 32), PLANE, 0, 0)

time: 83.6 us -> 79.5 us (0.951)
  Pallas kernels: 13.7 us -> 10.4 us
    pallas_call x2, Pallas kernels: 4.65 us -> 2.81 us  [the longest x1 1.66 us: basis(): call(basis_kernel, [(512, 128), (256, 512)], [VMEM] * 4, name='basis')]
    pallas_call x1, Pallas kernels: 8.98 us -> 7.47 us  [solve(): call(solve_kernel, [(64, 256), (64, 256)], [VMEM, VMEM], name='solve')]
where the time goes in v3:
time: 79.5 us; the launch traced here: 79.2 us
  blocking collectives  48.1 us (61%)
  starting transfers between devices  18.9 us (24%)
  Pallas kernels  10.4 us (13%)
  waiting for transfers between devices  1.13 us (1%)
    all_to_all x1, blocking collectives, shards(): parts = lax.all_to_all(total(parts, 16), 'z', 0, 0)  20.4 us
    all_to_all x1, blocking collectives, shards(): sums = lax.all_to_all(total(parts, 32), PLANE, 0, 0)  15.1 us
    ppermute x1, starting transfers between devices, shards(): pair = lax.ppermute(own, AXES, [(i, i ^ 1) for i in range(devices)])  14.4 us
    all_to_all x1, blocking collectives, shards(): parts = lax.all_to_all(sums.reshape(32, 16, 128), PLANE, 0, 0)  12.6 us
    pallas_call x1, Pallas kernels, solve(): call(solve_kernel, [(64, 256), (64, 256)], [VMEM, VMEM], name='solve')  7.47 us
    ppermute x1, starting transfers between devices, shards(): lax.ppermute(own, AXES, [(i, (i - 1 ^ 1) + 1 if i else devices - 1) if i...  4.5 us
    pallas_call x1, Pallas kernels, basis(): call(basis_kernel, [(512, 128), (256, 512)], [VMEM] * 4, name='basis')  1.66 us
  transfers between devices with their start and end apart: 2, of which 1 were waited for; matrix products, arithmetic and copies ran while one was open for 0% of the time, Pallas kernels for 0%

profile of v3, /device:TPU:1, one launch (start us, length us, event | category | flops | bytes accessed | tf_op | source)
XLA Modules:
  0.0 79.2 jit_solution(12227939007025654254)
XLA Ops:
  0.6 1.1 %pack.1 = (f32[256,256]{1,0:T(8,128)S(1)}, f32[8,128]{1,0:T(8,128)S(1)}) custom-call(s32[4,7]{1,0:T(4,128)} %bitcast.5, f32[64,256]{1,0:T(8,128)} %right_ref.1, f32[7,64,256]{2,1,0:T(8,128)} %blocks_ref.1), custom_call_target="tpu_custom_call" | custom-call | tf_op jit(solution)/shard_map/pack/pallas_call | solution.py:247
  1.8 4.5 %collective-permute-start.1 = (f32[256,256]{1,0:T(8,128)S(1)}, f32[256,256]{1,0:T(8,128)S(1)}, u32[]{:S(2)}, u32[]{:S(2)}) collective-permute-start(f32[256,256]{1,0:T(8,128)S(1)} %get-tuple-element.7.own_ref), channel_id=1, source_target_pairs={{0,511},{1,2},{2,1},{3,4},{4,3},{5,6},{6,5},{7,8},{8,7},{9,10},{10... | collective-permute-start | bytes 786440 | tf_op jit(solution)/shard_map/ppermute | solution.py:272
  6.3 14.4 %collective-permute-start = (f32[256,256]{1,0:T(8,128)S(1)}, f32[256,256]{1,0:T(8,128)S(1)}, u32[]{:S(2)}, u32[]{:S(2)}) collective-permute-start(f32[256,256]{1,0:T(8,128)S(1)} %get-tuple-element.7.own_ref), channel_id=1, source_target_pairs={{0,1},{1,0},{2,3},{3,2},{4,5},{5,4},{6,7},{7,6},{8,9},{9,8},{10,11... | collective-permute-start | bytes 786440 | tf_op jit(solution)/shard_map/ppermute | solution.py:271
  20.7 0.0 collective-permute-done.1.other_ref
  20.7 1.1 %collective-permute-done.pair_ref = f32[256,256]{1,0:T(8,128)S(1)} collective-permute-done((f32[256,256]{1,0:T(8,128)S(1)}, f32[256,256]{1,0:T(8,128)S(1)}, u32[]{:S(2)}, u32[]{:S(2)}) %collective-permute-start) | collective-permute-done | bytes 262176 | tf_op jit(solution)/shard_map/ppermute | solution.py:271
  21.8 1.7 %basis.1 = (f32[512,128]{1,0:T(8,128)S(1)}, f32[256,512]{1,0:T(8,128)S(1)}) custom-call(f32[8,128]{1,0:T(8,128)S(1)} %get-tuple-element.6.flag_ref, f32[256,256]{1,0:T(8,128)S(1)} %get-tuple-element.7.own_ref, f32[256,256]{1,0:T(8,128)S(1)} %collective-permute-done.pair_ref, f32[256,256]{1,0:T(8,128)S(1)} %collective-permute-done.1.other_ref), custom_call_target="tpu_custom_call" | custom-call | tf_op jit(solution)/shard_map/basis/pallas_call | solution.py:251
  23.5 12.6 %all_to_all.15.in_ref = f32[32,16,128]{2,1,0:T(8,128)S(1)} all-to-all(f32[32,16,128]{2,1,0:T(8,128)S(1)} %bitcast.4), channel_id=1, replica_groups=mesh['y'=4,'z'=16,'x'=4,'core'=2] {'y','x','core'}, dimensions={0} | all-to-all | bytes 524288 | tf_op jit(solution)/shard_map/all_to_all | solution.py:274
  36.2 20.4 %all_to_all.16.in_ref = f32[16,16,128]{2,1,0:T(8,128)S(1)} all-to-all(f32[16,16,128]{2,1,0:T(8,128)S(1)} %total.2), channel_id=1, replica_groups=mesh['y'=4,'z'=16,'x'=4,'core'=2] {'z'}, dimensions={0} | all-to-all | bytes 262144 | tf_op jit(solution)/shard_map/all_to_all | solution.py:275
  56.6 15.1 %all_to_all.17 = f32[32,16,128]{2,1,0:T(8,128)S(1)} all-to-all(f32[32,16,128]{2,1,0:T(8,128)S(1)} %total.3), channel_id=1, replica_groups=mesh['y'=4,'z'=16,'x'=4,'core'=2] {'y','x','core'}, dimensions={0} | all-to-all | bytes 524288 | tf_op jit(solution)/shard_map/all_to_all | solution.py:276
  71.7 7.5 %solve.1 = (f32[64,256]{1,0:T(8,128)}, f32[64,256]{1,0:T(8,128)}) custom-call(f32[512,128]{1,0:T(8,128)S(1)} %bitcast.3, f32[256,512]{1,0:T(8,128)S(1)} %get-tuple-element.9.stack_ref), custom_call_target="tpu_custom_call" | custom-call | tf_op jit(solution)/shard_map/solve/pallas_call | solution.py:260
  (2 shorter events, 0.1 us)
Async XLA Ops:
  1.8 18.9 %collective-permute-start.1 = (f32[256,256]{1,0:T(8,128)S(1)}, f32[256,256]{1,0:T(8,128)S(1)}, u32[]{:S(2)}, u32[]{:S(2)}) collective-permute-start(f32[256,256]{1,0:T(8,128)S(1)} %get-tuple-element.7.own_ref), channel_id=1, source_target_pairs={{0,511},{1,2},{2,1},{3,4},{4,3},{5,6},{6,5},{7,8},{8,7},{9,10},{10... | collective-permute-start | bytes 786440 | tf_op jit(solution)/shard_map/ppermute | solution.py:272
  6.3 15.5 %collective-permute-start = (f32[256,256]{1,0:T(8,128)S(1)}, f32[256,256]{1,0:T(8,128)S(1)}, u32[]{:S(2)}, u32[]{:S(2)}) collective-permute-start(f32[256,256]{1,0:T(8,128)S(1)} %get-tuple-element.7.own_ref), channel_id=1, source_target_pairs={{0,1},{1,0},{2,3},{3,2},{4,5},{5,4},{6,7},{7,6},{8,9},{9,8},{10,11... | collective-permute-start | bytes 786440 | tf_op jit(solution)/shard_map/ppermute | solution.py:271

commit v4 on v3

--- a/solution.py
+++ b/solution.py
@@ -16,7 +16,28 @@
 SMEM = pl.BlockSpec(memory_space=pltpu.SMEM)
 
 
-def pack_kernel(total_blocks, cols_hbm, right_ref, blocks_ref, out_ref, flag_ref, cols_ref, part_ref, cols_sem, part_sem, right_sem):
+def halves(a):
+    high = a.astype(jnp.bfloat16)
+    return high, (a - high.astype(jnp.float32)).astype(jnp.bfloat16)
+
+
+def product(a, b, dims):
+    one = lambda x, y: lax.dot_general(x, y, (dims, ((), ())), preferred_element_type=jnp.float32)
+    return one(a[0], b[0]) + (one(a[0], b[1]) + one(a[1], b[0]))
+
+
+def banded(minus, zero, plus):
+    left = lax.broadcasted_iota(jnp.int32, (BS, 128), 1) < BS
+    parts = [
+        jnp.where(left, minus, 0.0),
+        jnp.where(left, zero, minus),
+        jnp.where(left, plus, zero),
+        jnp.where(left, 0.0, plus),
+    ]
+    return halves(SCALE * jnp.concatenate(parts, axis=0))
+
+
+def pack_kernel(total_blocks, cols_hbm, right_ref, blocks_ref, out_ref, other_ref, pair_ref, flag_ref, cols_ref, part_ref, cols_sem, part_sem, right_sem):
     slots, _, width = part_ref.shape
     table = pltpu.make_async_copy(cols_hbm, cols_ref, cols_sem)
     table.start()
@@ -40,64 +61,48 @@
         offsets.append(offset)
     for copy in copies:
         copy.wait()
+    inner = []
     for at, value, fixed in ((0, -1, (2, 4)), (64, 0, (0,)), (128, 1, (1, 3))):
         kept = sum(part_ref[slot] for slot in fixed)
         for slot, offset in zip((5, 6), offsets):
             kept = kept + jnp.where(offset == value, part_ref[slot], 0.0)
         out_ref[at : at + 64, :] = kept
+        inner.append(pltpu.roll(kept, 64, 1)[:, 128:256])
     last.wait()
-
-
-def halves(a):
-    high = a.astype(jnp.bfloat16)
-    return high, (a - high.astype(jnp.float32)).astype(jnp.bfloat16)
-
-
-def product(a, b, dims):
-    one = lambda x, y: lax.dot_general(x, y, (dims, ((), ())), preferred_element_type=jnp.float32)
-    return one(a[0], b[0]) + (one(a[0], b[1]) + one(a[1], b[0]))
-
-
-def basis_kernel(flag_ref, own_ref, pair_ref, other_ref, sums_ref, stack_ref):
+    image = product(halves(out_ref[192:256, :]), banded(*inner), ((1,), (0,)))
+    even = jnp.full((1, 128), odd, jnp.int32) == 0
+    head, tail = out_ref[:, 0:128], out_ref[:, 128:256]
+    pair_ref[0:256, :] = jnp.where(even, tail, head)
+    other_ref[0:256, :] = jnp.where(even, head, tail)
+    pair_ref[256:320, :] = image
+    other_ref[256:320, :] = image
+
+
+def basis_kernel(flag_ref, own_ref, other_ref, pair_ref, sums_ref, stack_ref):
     even = flag_ref[0:1, :] > 0
-    left = lax.broadcasted_iota(jnp.int32, (BS, 128), 1) < BS
-    bands, tiles = [], []
-    for p in range(6):
-        at = slice(128 * (p % 2), 128 * (p % 2 + 1))
-        if p < 2:
-            get = lambda r: jnp.where(even, other_ref[r, at], pair_ref[r, at])
-        elif p < 4:
-            get = lambda r: own_ref[r, at]
-        else:
-            get = lambda r: jnp.where(even, pair_ref[r, at], other_ref[r, at])
-        minus, zero, plus = get(slice(0, 64)), get(slice(64, 128)), get(slice(128, 192))
-        band = jnp.concatenate(
-            [
-                jnp.where(left, minus, 0.0),
-                jnp.where(left, zero, minus),
-                jnp.where(left, plus, zero),
-                jnp.where(left, 0.0, plus),
-            ],
-            axis=0,
-        )
-        bands.append(halves(SCALE * band))
-        tiles.append(get(slice(192, 256)))
-    own = [jnp.concatenate(tiles[2:4], axis=1)]
-    first = 0
-    for low, high in ((0, 6), (1, 5), (1, 5), (2, 4)):
-        current = jnp.concatenate(tiles, axis=1)
-        rolled = halves(pltpu.roll(current, 64, 1))
-        fresh = []
-        for p in range(low, high):
-            at = 128 * (p - first)
-            if at + 256 <= current.shape[1]:
-                window = [r[:, at : at + 256] for r in rolled]
-            else:
-                window = [jnp.concatenate([r[:, at:], r[:, :128]], axis=1) for r in rolled]
-            fresh.append(product(window, bands[p], ((1,), (0,))))
-        own.append(jnp.concatenate(fresh[2 - low : 4 - low], axis=1))
+    pair, other = pair_ref[...], other_ref[...]
+    ends = jnp.where(even, other, pair), jnp.where(even, pair, other)
+    parts = [ends[0], own_ref[:, 0:128], own_ref[:, 128:256], ends[1]]
+    bands = [banded(part[0:64], part[64:128], part[128:192]) for part in parts]
+    edges = [halves(end[256:320]) for end in ends]
+
+    def rolled(tiles):
+        both = halves(pltpu.roll(jnp.concatenate(tiles, axis=1), 64, 1))
+        shifted = [tuple(r[:, 128 * p : 128 * (p + 1)] for r in both) for p in range(4)]
+        return shifted + shifted[:1]
+
+    tiles = [part[192:256] for part in parts]
+    own = [jnp.concatenate(tiles[1:3], axis=1)]
+    for step in range(S):
+        shifted = rolled(tiles)
+        if step == 1:
+            shifted[0], shifted[4] = edges
+        fresh = list(tiles)
+        for p in range(4) if step < S - 1 else (1, 2):
+            window = [jnp.concatenate([a, b], axis=1) for a, b in zip(shifted[p], shifted[p + 1])]
+            fresh[p] = product(window, bands[p], ((1,), (0,)))
         tiles = fresh
-        first = low
+        own.append(jnp.concatenate(tiles[1:3], axis=1))
     images = [own[k] + own[k + 1] / SCALE for k in range(S)]
     w = jnp.concatenate(images, axis=0)
     stack_ref[:, 0:256] = jnp.concatenate(own[:S], axis=0)
@@ -244,11 +249,11 @@
         pltpu.SemaphoreType.DMA,
     )
     arrays = [pltpu.with_memory_space_constraint(a, pltpu.HBM) for a in (cols, right_side, blocks)]
-    return call(kernel, [(256, 256), (8, 128)], [HBM] * 3, scratch, name="pack")(*arrays)
-
-
-def basis(flag, own, pair, other):
-    return call(basis_kernel, [(512, 128), (256, 512)], [VMEM] * 4, name="basis")(flag, own, pair, other)
+    return call(kernel, [(256, 256), (320, 128), (320, 128), (8, 128)], [HBM] * 3, scratch, name="pack")(*arrays)
+
+
+def basis(flag, own, other, pair):
+    return call(basis_kernel, [(512, 128), (256, 512)], [VMEM] * 4, name="basis")(flag, own, other, pair)
 
 
 def total(parts, copies):
@@ -267,10 +272,10 @@
 def shards(right_side, blocks, cols):
     devices = lax.axis_size(AXES)
     cols = cols.T
-    own, flag = pack(cols, right_side, blocks, cols.shape[0] * devices)
-    pair = lax.ppermute(own, AXES, [(i, i ^ 1) for i in range(devices)])
-    other = lax.ppermute(own, AXES, [(i, ((i - 1) ^ 1) + 1 if i else devices - 1) if i < devices - 1 else (i, 0) for i in range(devices)])
-    sums, stack = basis(flag, own, pair, other)
+    own, other, pair, flag = pack(cols, right_side, blocks, cols.shape[0] * devices)
+    other = lax.ppermute(other, AXES, [(i, ((i - 1) ^ 1) + 1) if 0 < i < devices - 1 else (i, devices - 1 - i) for i in range(devices)])
+    pair = lax.ppermute(pair, AXES, [(i, i ^ 1) for i in range(devices)])
+    sums, stack = basis(flag, own, other, pair)
     parts = lax.all_to_all(sums.reshape(32, 16, 128), PLANE, 0, 0)
     parts = lax.all_to_all(total(parts, 16), "z", 0, 0)
     sums = lax.all_to_all(total(parts, 32), PLANE, 0, 0)

time: 79.5 us -> 78.7 us (0.990)
  blocking collectives: 48.1 us -> 47.2 us
where the time goes in v4:
time: 78.7 us; the launch traced here: 78.4 us
  blocking collectives  47.2 us (60%)
  starting transfers between devices  18.9 us (24%)
  Pallas kernels  10.6 us (13%)
  waiting for transfers between devices  1 us (1%)
    all_to_all x1, blocking collectives, shards(): parts = lax.all_to_all(total(parts, 16), 'z', 0, 0)  20.1 us
    all_to_all x1, blocking collectives, shards(): sums = lax.all_to_all(total(parts, 32), PLANE, 0, 0)  15.1 us
    ppermute x1, starting transfers between devices, shards(): pair = lax.ppermute(pair, AXES, [(i, i ^ 1) for i in range(devices)])  14.4 us
    all_to_all x1, blocking collectives, shards(): parts = lax.all_to_all(sums.reshape(32, 16, 128), PLANE, 0, 0)  12 us
    pallas_call x1, Pallas kernels, solve(): call(solve_kernel, [(64, 256), (64, 256)], [VMEM, VMEM], name='solve')  7.47 us
    ppermute x1, starting transfers between devices, shards(): lax.ppermute(other, AXES, [(i, (i - 1 ^ 1) + 1) if 0 < i < devices - 1 el...  4.5 us
    pallas_call x1, Pallas kernels, basis(): call(basis_kernel, [(512, 128), (256, 512)], [VMEM] * 4, name='basis')  1.62 us
  transfers between devices with their start and end apart: 2, of which 1 were waited for; matrix products, arithmetic and copies ran while one was open for 0% of the time, Pallas kernels for 0%

profile of v4, /device:TPU:1, one launch (start us, length us, event | category | flops | bytes accessed | tf_op | source)
XLA Modules:
  0.0 78.4 jit_solution(1721679970665408228)
XLA Ops:
  0.6 1.4 %pack.1 = (f32[256,256]{1,0:T(8,128)S(1)}, f32[320,128]{1,0:T(8,128)S(1)}, f32[320,128]{1,0:T(8,128)S(1)}, f32[8,128]{1,0:T(8,128)S(1)}) custom-call(s32[4,7]{1,0:T(4,128)} %bitcast.5, f32[64,256]{1,0:T(8,128)} %right_ref.1, f32[7,64,256]{2,1,0:T(8,128)} %blocks_ref.1), custom_call_target="tpu_custom_call" | custom-call | tf_op jit(solution)/shard_map/pack/pallas_call | solution.py:252
  2.1 4.5 %collective-permute-start = (f32[320,128]{1,0:T(8,128)S(1)}, f32[320,128]{1,0:T(8,128)S(1)}, u32[]{:S(2)}, u32[]{:S(2)}) collective-permute-start(f32[320,128]{1,0:T(8,128)S(1)} %get-tuple-element.10), channel_id=1, source_target_pairs={{0,511},{1,2},{2,1},{3,4},{4,3},{5,6},{6,5},{7,8},{8,7},{9,10},{10... | collective-permute-start | bytes 491528 | tf_op jit(solution)/shard_map/ppermute | solution.py:276
  6.6 14.4 %collective-permute-start.1 = (f32[320,128]{1,0:T(8,128)S(1)}, f32[320,128]{1,0:T(8,128)S(1)}, u32[]{:S(2)}, u32[]{:S(2)}) collective-permute-start(f32[320,128]{1,0:T(8,128)S(1)} %get-tuple-element.11), channel_id=1, source_target_pairs={{0,1},{1,0},{2,3},{3,2},{4,5},{5,4},{6,7},{7,6},{8,9},{9,8},{10,11... | collective-permute-start | bytes 491528 | tf_op jit(solution)/shard_map/ppermute | solution.py:277
  21.0 0.0 collective-permute-done.other_ref
  21.0 1.0 %collective-permute-done.1.pair_ref = f32[320,128]{1,0:T(8,128)S(1)} collective-permute-done((f32[320,128]{1,0:T(8,128)S(1)}, f32[320,128]{1,0:T(8,128)S(1)}, u32[]{:S(2)}, u32[]{:S(2)}) %collective-permute-start.1) | collective-permute-done | bytes 163872 | tf_op jit(solution)/shard_map/ppermute | solution.py:277
  22.0 1.6 %basis.1 = (f32[512,128]{1,0:T(8,128)S(1)}, f32[256,512]{1,0:T(8,128)S(1)}) custom-call(f32[8,128]{1,0:T(8,128)S(1)} %get-tuple-element.8.flag_ref, f32[256,256]{1,0:T(8,128)S(1)} %get-tuple-element.9.own_ref, f32[320,128]{1,0:T(8,128)S(1)} %collective-permute-done.other_ref, f32[320,128]{1,0:T(8,128)S(1)} %collective-permute-done.1.pair_ref), custom_call_target="tpu_custom_call" | custom-call | tf_op jit(solution)/shard_map/basis/pallas_call | solution.py:256
  23.6 12.0 %all_to_all.15.in_ref = f32[32,16,128]{2,1,0:T(8,128)S(1)} all-to-all(f32[32,16,128]{2,1,0:T(8,128)S(1)} %bitcast.4), channel_id=1, replica_groups=mesh['y'=4,'z'=16,'x'=4,'core'=2] {'y','x','core'}, dimensions={0} | all-to-all | bytes 524288 | tf_op jit(solution)/shard_map/all_to_all | solution.py:279
  35.6 20.1 %all_to_all.16.in_ref = f32[16,16,128]{2,1,0:T(8,128)S(1)} all-to-all(f32[16,16,128]{2,1,0:T(8,128)S(1)} %total.2), channel_id=1, replica_groups=mesh['y'=4,'z'=16,'x'=4,'core'=2] {'z'}, dimensions={0} | all-to-all | bytes 262144 | tf_op jit(solution)/shard_map/all_to_all | solution.py:280
  55.8 15.1 %all_to_all.17 = f32[32,16,128]{2,1,0:T(8,128)S(1)} all-to-all(f32[32,16,128]{2,1,0:T(8,128)S(1)} %total.3), channel_id=1, replica_groups=mesh['y'=4,'z'=16,'x'=4,'core'=2] {'y','x','core'}, dimensions={0} | all-to-all | bytes 524288 | tf_op jit(solution)/shard_map/all_to_all | solution.py:281
  70.9 7.5 %solve.1 = (f32[64,256]{1,0:T(8,128)}, f32[64,256]{1,0:T(8,128)}) custom-call(f32[512,128]{1,0:T(8,128)S(1)} %bitcast.3, f32[256,512]{1,0:T(8,128)S(1)} %get-tuple-element.13.stack_ref), custom_call_target="tpu_custom_call" | custom-call | tf_op jit(solution)/shard_map/solve/pallas_call | solution.py:265
  (2 shorter events, 0.1 us)
Async XLA Ops:
  2.1 18.9 %collective-permute-start = (f32[320,128]{1,0:T(8,128)S(1)}, f32[320,128]{1,0:T(8,128)S(1)}, u32[]{:S(2)}, u32[]{:S(2)}) collective-permute-start(f32[320,128]{1,0:T(8,128)S(1)} %get-tuple-element.10), channel_id=1, source_target_pairs={{0,511},{1,2},{2,1},{3,4},{4,3},{5,6},{6,5},{7,8},{8,7},{9,10},{10... | collective-permute-start | bytes 491528 | tf_op jit(solution)/shard_map/ppermute | solution.py:276
  6.6 15.4 %collective-permute-start.1 = (f32[320,128]{1,0:T(8,128)S(1)}, f32[320,128]{1,0:T(8,128)S(1)}, u32[]{:S(2)}, u32[]{:S(2)}) collective-permute-start(f32[320,128]{1,0:T(8,128)S(1)} %get-tuple-element.11), channel_id=1, source_target_pairs={{0,1},{1,0},{2,3},{3,2},{4,5},{5,4},{6,7},{7,6},{8,9},{9,8},{10,11... | collective-permute-start | bytes 491528 | tf_op jit(solution)/shard_map/ppermute | solution.py:277

commit v5 on v4

--- a/solution.py
+++ b/solution.py
@@ -147,13 +147,16 @@
     for k in range(0, BS, 2):
         at, row = k // 8, k % 8
         first, second = ahead.pop(k), ahead.pop(k + 1)
-        a, b, d = first[at][row : row + 1, :], first[at][row + 1 : row + 2, :], second[at][row + 1 : row + 2, :]
+        up = lambda x: pltpu.roll(x, 7, 0)
+        a, b, d = first[at], second[at], up(second[at])
         inverse = 1.0 / (a * d - b * b)
-        p, q, r = d * inverse, -b * inverse, a * inverse
-
-        def solved(top, low):
-            n = top.shape[1]
-            return p[:, :n] * top + q[:, :n] * low, q[:, :n] * top + r[:, :n] * low
+        p, q, r = (x[row : row + 1, :] for x in (d * inverse, b * inverse, a * inverse))
+
+        def solved(x):
+            n = x.shape[1]
+            low, x = up(x)[row : row + 1, :], x[row : row + 1, :]
+            top, low = p[:, :n] * x - q[:, :n] * low, r[:, :n] * low - q[:, :n] * x
+            return top, low
 
         if row < 6:
             keep = rows > row + 1
@@ -162,12 +165,12 @@
         else:
             live = range(at + 1, groups)
         for column in ahead.values():
-            top, low = solved(column[at][row : row + 1, :], column[at][row + 1 : row + 2, :])
+            top, low = solved(column[at])
             for g in live:
                 if g in column:
                     column[g] = column[g] - (first[g] * top + second[g] * low)
         for t in range(tiles):
-            top, low = solved(part[at][t][row : row + 1, :], part[at][t][row + 1 : row + 2, :])
+            top, low = solved(part[at][t])
             n = top.shape[1]
             for g in live:
                 part[g][t] = part[g][t] - (first[g][:, :n] * top + second[g][:, :n] * low)
@@ -180,7 +183,7 @@
     return join(part), join(scaled)
 
 
-def solve_kernel(sums_ref, stack_ref, update_ref, residual_ref):
+def solve_kernel(sums_ref, stack_ref, update_hbm, residual_hbm, update_ref, residual_ref, update_sem, residual_sem):
     u = [sums_ref[64 * k : 64 * (k + 1), :] for k in range(7)]
     row = lax.broadcasted_iota(jnp.int32, (BS, 128), 0)
     lane = lax.broadcasted_iota(jnp.int32, (BS, 128), 1)
@@ -217,17 +220,23 @@
                     fresh.append(tile)
             tiles[i] = fresh
         solved = narrow(y[5], jnp.concatenate([z[n] for n in range(k + 1, 5)], axis=1), ((0,), (0,)))
-        term = narrow(solved[:, 64 * (S - 1 - k) :], spans[k], ((0,), (0,)))
-        both = term if both is None else both + term
+        term = [narrow(solved[:, 64 * (S - 1 - k) :], spans[k][:, 256 * h : 256 * (h + 1)], ((0,), (0,))) for h in (0, 1)]
+        both = term if both is None else [b + t for b, t in zip(both, term)]
         for i in range(k + 1, S):
             spans[i] = spans[i] - narrow(solved[:, 64 * (i - k - 1) : 64 * (i - k)], spans[k], ((0,), (0,)))
-    update_ref[...] = both[:, 0:256]
-    residual_ref[...] = stack_ref[0:64, 0:256] - both[:, 256:512]
-
-
-def call(kernel, outs, in_specs, scratch=(), name=None):
+    update_ref[...] = both[0]
+    update = pltpu.make_async_copy(update_ref, update_hbm, update_sem)
+    update.start()
+    residual_ref[...] = stack_ref[0:64, 0:256] - both[1]
+    residual = pltpu.make_async_copy(residual_ref, residual_hbm, residual_sem)
+    residual.start()
+    update.wait()
+    residual.wait()
+
+
+def call(kernel, outs, in_specs, scratch=(), name=None, space=VMEM):
     shapes = [jax.ShapeDtypeStruct(s, jnp.float32) for s in outs]
-    specs = [VMEM] * len(outs)
+    specs = [space] * len(outs)
     return pl.pallas_call(
         kernel,
         out_shape=shapes if len(outs) > 1 else shapes[0],
@@ -262,7 +271,8 @@
 
 
 def solve(sums, stack):
-    return call(solve_kernel, [(64, 256), (64, 256)], [VMEM, VMEM], name="solve")(sums, stack)
+    scratch = [pltpu.VMEM((64, 256), jnp.float32)] * 2 + [pltpu.SemaphoreType.DMA] * 2
+    return call(solve_kernel, [(64, 256), (64, 256)], [VMEM, VMEM], scratch, "solve", HBM)(sums, stack)
 
 
 AXES = ("y", "z", "x", "core")

time: 78.7 us -> 78.3 us (level)
  no operation moved by 1% of the time
where the time goes in v5:
time: 78.3 us; the launch traced here: 78 us
  blocking collectives  47.2 us (60%)
  starting transfers between devices  18.9 us (24%)
  Pallas kernels  10.2 us (13%)
  waiting for transfers between devices  1 us (1%)
    all_to_all x1, blocking collectives, shards(): parts = lax.all_to_all(total(parts, 16), 'z', 0, 0)  20.1 us
    all_to_all x1, blocking collectives, shards(): sums = lax.all_to_all(total(parts, 32), PLANE, 0, 0)  15.1 us
    ppermute x1, starting transfers between devices, shards(): pair = lax.ppermute(pair, AXES, [(i, i ^ 1) for i in range(devices)])  14.4 us
    all_to_all x1, blocking collectives, shards(): parts = lax.all_to_all(sums.reshape(32, 16, 128), PLANE, 0, 0)  12 us
    pallas_call x1, Pallas kernels, solve(): call(solve_kernel, [(64, 256), (64, 256)], [VMEM, VMEM], scratch, 'solve'...  7.08 us
    ppermute x1, starting transfers between devices, shards(): lax.ppermute(other, AXES, [(i, (i - 1 ^ 1) + 1) if 0 < i < devices - 1 el...  4.5 us
    pallas_call x1, Pallas kernels, basis(): call(basis_kernel, [(512, 128), (256, 512)], [VMEM] * 4, name='basis')  1.62 us
  transfers between devices with their start and end apart: 2, of which 1 were waited for; matrix products, arithmetic and copies ran while one was open for 0% of the time, Pallas kernels for 0%

profile of v5, /device:TPU:1, one launch (start us, length us, event | category | flops | bytes accessed | tf_op | source)
XLA Modules:
  0.0 78.0 jit_solution(91658894951229942)
XLA Ops:
  0.6 1.4 %pack.1 = (f32[256,256]{1,0:T(8,128)S(1)}, f32[320,128]{1,0:T(8,128)S(1)}, f32[320,128]{1,0:T(8,128)S(1)}, f32[8,128]{1,0:T(8,128)S(1)}) custom-call(s32[4,7]{1,0:T(4,128)} %bitcast.5, f32[64,256]{1,0:T(8,128)} %right_ref.1, f32[7,64,256]{2,1,0:T(8,128)} %blocks_ref.1), custom_call_target="tpu_custom_call" | custom-call | tf_op jit(solution)/shard_map/pack/pallas_call | solution.py:261
  2.1 4.5 %collective-permute-start = (f32[320,128]{1,0:T(8,128)S(1)}, f32[320,128]{1,0:T(8,128)S(1)}, u32[]{:S(2)}, u32[]{:S(2)}) collective-permute-start(f32[320,128]{1,0:T(8,128)S(1)} %get-tuple-element.10), channel_id=1, source_target_pairs={{0,511},{1,2},{2,1},{3,4},{4,3},{5,6},{6,5},{7,8},{8,7},{9,10},{10... | collective-permute-start | bytes 491528 | tf_op jit(solution)/shard_map/ppermute | solution.py:286
  6.6 14.4 %collective-permute-start.1 = (f32[320,128]{1,0:T(8,128)S(1)}, f32[320,128]{1,0:T(8,128)S(1)}, u32[]{:S(2)}, u32[]{:S(2)}) collective-permute-start(f32[320,128]{1,0:T(8,128)S(1)} %get-tuple-element.11), channel_id=1, source_target_pairs={{0,1},{1,0},{2,3},{3,2},{4,5},{5,4},{6,7},{7,6},{8,9},{9,8},{10,11... | collective-permute-start | bytes 491528 | tf_op jit(solution)/shard_map/ppermute | solution.py:287
  21.0 0.0 collective-permute-done.other_ref
  21.0 1.0 %collective-permute-done.1.pair_ref = f32[320,128]{1,0:T(8,128)S(1)} collective-permute-done((f32[320,128]{1,0:T(8,128)S(1)}, f32[320,128]{1,0:T(8,128)S(1)}, u32[]{:S(2)}, u32[]{:S(2)}) %collective-permute-start.1) | collective-permute-done | bytes 163872 | tf_op jit(solution)/shard_map/ppermute | solution.py:287
  22.0 1.6 %basis.1 = (f32[512,128]{1,0:T(8,128)S(1)}, f32[256,512]{1,0:T(8,128)S(1)}) custom-call(f32[8,128]{1,0:T(8,128)S(1)} %get-tuple-element.8.flag_ref, f32[256,256]{1,0:T(8,128)S(1)} %get-tuple-element.9.own_ref, f32[320,128]{1,0:T(8,128)S(1)} %collective-permute-done.other_ref, f32[320,128]{1,0:T(8,128)S(1)} %collective-permute-done.1.pair_ref), custom_call_target="tpu_custom_call" | custom-call | tf_op jit(solution)/shard_map/basis/pallas_call | solution.py:265
  23.6 12.0 %all_to_all.15.in_ref = f32[32,16,128]{2,1,0:T(8,128)S(1)} all-to-all(f32[32,16,128]{2,1,0:T(8,128)S(1)} %bitcast.4), channel_id=1, replica_groups=mesh['y'=4,'z'=16,'x'=4,'core'=2] {'y','x','core'}, dimensions={0} | all-to-all | bytes 524288 | tf_op jit(solution)/shard_map/all_to_all | solution.py:289
  35.6 20.1 %all_to_all.16.in_ref = f32[16,16,128]{2,1,0:T(8,128)S(1)} all-to-all(f32[16,16,128]{2,1,0:T(8,128)S(1)} %total.2), channel_id=1, replica_groups=mesh['y'=4,'z'=16,'x'=4,'core'=2] {'z'}, dimensions={0} | all-to-all | bytes 262144 | tf_op jit(solution)/shard_map/all_to_all | solution.py:290
  55.8 15.1 %all_to_all.17 = f32[32,16,128]{2,1,0:T(8,128)S(1)} all-to-all(f32[32,16,128]{2,1,0:T(8,128)S(1)} %total.3), channel_id=1, replica_groups=mesh['y'=4,'z'=16,'x'=4,'core'=2] {'y','x','core'}, dimensions={0} | all-to-all | bytes 524288 | tf_op jit(solution)/shard_map/all_to_all | solution.py:291
  70.9 7.1 %solve.1 = (f32[64,256]{1,0:T(8,128)}, f32[64,256]{1,0:T(8,128)}) custom-call(f32[512,128]{1,0:T(8,128)S(1)} %bitcast.3, f32[256,512]{1,0:T(8,128)S(1)} %get-tuple-element.13.stack_ref), custom_call_target="tpu_custom_call" | custom-call | tf_op jit(solution)/shard_map/solve/pallas_call | solution.py:275
  (2 shorter events, 0.1 us)
Async XLA Ops:
  2.1 18.9 %collective-permute-start = (f32[320,128]{1,0:T(8,128)S(1)}, f32[320,128]{1,0:T(8,128)S(1)}, u32[]{:S(2)}, u32[]{:S(2)}) collective-permute-start(f32[320,128]{1,0:T(8,128)S(1)} %get-tuple-element.10), channel_id=1, source_target_pairs={{0,511},{1,2},{2,1},{3,4},{4,3},{5,6},{6,5},{7,8},{8,7},{9,10},{10... | collective-permute-start | bytes 491528 | tf_op jit(solution)/shard_map/ppermute | solution.py:286
  6.6 15.4 %collective-permute-start.1 = (f32[320,128]{1,0:T(8,128)S(1)}, f32[320,128]{1,0:T(8,128)S(1)}, u32[]{:S(2)}, u32[]{:S(2)}) collective-permute-start(f32[320,128]{1,0:T(8,128)S(1)} %get-tuple-element.11), channel_id=1, source_target_pairs={{0,1},{1,0},{2,3},{3,2},{4,5},{5,4},{6,7},{7,6},{8,9},{9,8},{10,11... | collective-permute-start | bytes 491528 | tf_op jit(solution)/shard_map/ppermute | solution.py:287

commit v6 on v5

--- a/solution.py
+++ b/solution.py
@@ -275,8 +275,8 @@
     return call(solve_kernel, [(64, 256), (64, 256)], [VMEM, VMEM], scratch, "solve", HBM)(sums, stack)
 
 
-AXES = ("y", "z", "x", "core")
-PLANE = ("y", "x", "core")
+AXES = ("y", "z", "next", "x", "core")
+NEAR = ("y", "next", "x", "core")
 
 
 def shards(right_side, blocks, cols):
@@ -286,14 +286,14 @@
     other = lax.ppermute(other, AXES, [(i, ((i - 1) ^ 1) + 1) if 0 < i < devices - 1 else (i, devices - 1 - i) for i in range(devices)])
     pair = lax.ppermute(pair, AXES, [(i, i ^ 1) for i in range(devices)])
     sums, stack = basis(flag, own, other, pair)
-    parts = lax.all_to_all(sums.reshape(32, 16, 128), PLANE, 0, 0)
-    parts = lax.all_to_all(total(parts, 16), "z", 0, 0)
-    sums = lax.all_to_all(total(parts, 32), PLANE, 0, 0)
+    parts = lax.all_to_all(sums.reshape(64, 8, 128), NEAR, 0, 0)
+    parts = lax.all_to_all(total(parts, 8), "z", 0, 0)
+    sums = lax.all_to_all(total(parts, 64), NEAR, 0, 0)
     return tuple(solve(sums.reshape(512, 128), stack))
 
 
 def solution(mesh):
-    grid = Mesh(mesh.devices.reshape(4, 16, 4, 2), AXES)
+    grid = Mesh(mesh.devices.reshape(4, 8, 2, 4, 2), AXES)
     in_specs = (P(None, AXES), P(None, None, AXES), P(None, AXES))
     out_specs = (P(None, AXES), P(None, AXES))
     return jax.shard_map(shards, mesh=grid, in_specs=in_specs, out_specs=out_specs, check_vma=False)

time: 78.3 us -> 80.4 us (1.027)
  blocking collectives: 47.2 us -> 49.3 us
    all_to_all x3, blocking collectives: 47.2 us -> 49.3 us  [the longest x1 20.5 us: shards(): parts = lax.all_to_all(total(parts, 8), 'z', 0, 0)]
where the time goes in v6:
time: 80.4 us; the launch traced here: 80 us
  blocking collectives  49.3 us (61%)
  starting transfers between devices  18.9 us (24%)
  Pallas kernels  10.2 us (13%)
  waiting for transfers between devices  1 us (1%)
    all_to_all x1, blocking collectives, shards(): parts = lax.all_to_all(total(parts, 8), 'z', 0, 0)  20.5 us
    all_to_all x1, blocking collectives, shards(): sums = lax.all_to_all(total(parts, 64), NEAR, 0, 0)  15.3 us
    ppermute x1, starting transfers between devices, shards(): pair = lax.ppermute(pair, AXES, [(i, i ^ 1) for i in range(devices)])  14.4 us
    all_to_all x1, blocking collectives, shards(): parts = lax.all_to_all(sums.reshape(64, 8, 128), NEAR, 0, 0)  13.5 us
    pallas_call x1, Pallas kernels, solve(): call(solve_kernel, [(64, 256), (64, 256)], [VMEM, VMEM], scratch, 'solve'...  7.09 us
    ppermute x1, starting transfers between devices, shards(): lax.ppermute(other, AXES, [(i, (i - 1 ^ 1) + 1) if 0 < i < devices - 1 el...  4.5 us
    pallas_call x1, Pallas kernels, basis(): call(basis_kernel, [(512, 128), (256, 512)], [VMEM] * 4, name='basis')  1.62 us
  transfers between devices with their start and end apart: 2, of which 1 were waited for; matrix products, arithmetic and copies ran while one was open for 0% of the time, Pallas kernels for 0%

profile of v6, /device:TPU:1, one launch (start us, length us, event | category | flops | bytes accessed | tf_op | source)
XLA Modules:
  0.0 80.0 jit_solution(4561472266988639562)
XLA Ops:
  0.6 1.4 %pack.1 = (f32[256,256]{1,0:T(8,128)S(1)}, f32[320,128]{1,0:T(8,128)S(1)}, f32[320,128]{1,0:T(8,128)S(1)}, f32[8,128]{1,0:T(8,128)S(1)}) custom-call(s32[4,7]{1,0:T(4,128)} %bitcast.5, f32[64,256]{1,0:T(8,128)} %right_ref.1, f32[7,64,256]{2,1,0:T(8,128)} %blocks_ref.1), custom_call_target="tpu_custom_call" | custom-call | tf_op jit(solution)/shard_map/pack/pallas_call | solution.py:261
  2.1 4.5 %collective-permute-start = (f32[320,128]{1,0:T(8,128)S(1)}, f32[320,128]{1,0:T(8,128)S(1)}, u32[]{:S(2)}, u32[]{:S(2)}) collective-permute-start(f32[320,128]{1,0:T(8,128)S(1)} %get-tuple-element.10), channel_id=1, source_target_pairs={{0,511},{1,2},{2,1},{3,4},{4,3},{5,6},{6,5},{7,8},{8,7},{9,10},{10... | collective-permute-start | bytes 491528 | tf_op jit(solution)/shard_map/ppermute | solution.py:286
  6.6 14.4 %collective-permute-start.1 = (f32[320,128]{1,0:T(8,128)S(1)}, f32[320,128]{1,0:T(8,128)S(1)}, u32[]{:S(2)}, u32[]{:S(2)}) collective-permute-start(f32[320,128]{1,0:T(8,128)S(1)} %get-tuple-element.11), channel_id=1, source_target_pairs={{0,1},{1,0},{2,3},{3,2},{4,5},{5,4},{6,7},{7,6},{8,9},{9,8},{10,11... | collective-permute-start | bytes 491528 | tf_op jit(solution)/shard_map/ppermute | solution.py:287
  21.0 0.0 collective-permute-done.other_ref
  21.0 1.0 %collective-permute-done.1.pair_ref = f32[320,128]{1,0:T(8,128)S(1)} collective-permute-done((f32[320,128]{1,0:T(8,128)S(1)}, f32[320,128]{1,0:T(8,128)S(1)}, u32[]{:S(2)}, u32[]{:S(2)}) %collective-permute-start.1) | collective-permute-done | bytes 163872 | tf_op jit(solution)/shard_map/ppermute | solution.py:287
  22.0 1.6 %basis.1 = (f32[512,128]{1,0:T(8,128)S(1)}, f32[256,512]{1,0:T(8,128)S(1)}) custom-call(f32[8,128]{1,0:T(8,128)S(1)} %get-tuple-element.8.flag_ref, f32[256,256]{1,0:T(8,128)S(1)} %get-tuple-element.9.own_ref, f32[320,128]{1,0:T(8,128)S(1)} %collective-permute-done.other_ref, f32[320,128]{1,0:T(8,128)S(1)} %collective-permute-done.1.pair_ref), custom_call_target="tpu_custom_call" | custom-call | tf_op jit(solution)/shard_map/basis/pallas_call | solution.py:265
  23.6 13.5 %all_to_all.15.in_ref = f32[64,8,128]{2,1,0:T(8,128)S(1)} all-to-all(f32[64,8,128]{2,1,0:T(8,128)S(1)} %bitcast.4), channel_id=1, replica_groups=mesh['y'=4,'z'=8,'next'=2,'x'=4,'core'=2] {'y','next','x','core'}, dimensions={0} | all-to-all | bytes 524288 | tf_op jit(solution)/shard_map/all_to_all | solution.py:289
  37.1 0.1 total.2
  37.2 20.5 %all_to_all.16.in_ref = f32[8,8,128]{2,1,0:T(8,128)S(1)} all-to-all(f32[8,8,128]{2,1,0:T(8,128)S(1)} %total.2), channel_id=1, replica_groups=mesh['y'=4,'z'=8,'next'=2,'x'=4,'core'=2] {'z'}, dimensions={0} | all-to-all | bytes 65536 | tf_op jit(solution)/shard_map/all_to_all | solution.py:290
  57.7 15.3 %all_to_all.17 = f32[64,8,128]{2,1,0:T(8,128)S(1)} all-to-all(f32[64,8,128]{2,1,0:T(8,128)S(1)} %total.3), channel_id=1, replica_groups=mesh['y'=4,'z'=8,'next'=2,'x'=4,'core'=2] {'y','next','x','core'}, dimensions={0} | all-to-all | bytes 524288 | tf_op jit(solution)/shard_map/all_to_all | solution.py:291
  72.9 7.1 %solve.1 = (f32[64,256]{1,0:T(8,128)}, f32[64,256]{1,0:T(8,128)}) custom-call(f32[512,128]{1,0:T(8,128)S(1)} %bitcast.3, f32[256,512]{1,0:T(8,128)S(1)} %get-tuple-element.13.stack_ref), custom_call_target="tpu_custom_call" | custom-call | tf_op jit(solution)/shard_map/solve/pallas_call | solution.py:275
  (1 shorter events, 0.0 us)
Async XLA Ops:
  2.1 18.9 %collective-permute-start = (f32[320,128]{1,0:T(8,128)S(1)}, f32[320,128]{1,0:T(8,128)S(1)}, u32[]{:S(2)}, u32[]{:S(2)}) collective-permute-start(f32[320,128]{1,0:T(8,128)S(1)} %get-tuple-element.10), channel_id=1, source_target_pairs={{0,511},{1,2},{2,1},{3,4},{4,3},{5,6},{6,5},{7,8},{8,7},{9,10},{10... | collective-permute-start | bytes 491528 | tf_op jit(solution)/shard_map/ppermute | solution.py:286
  6.6 15.4 %collective-permute-start.1 = (f32[320,128]{1,0:T(8,128)S(1)}, f32[320,128]{1,0:T(8,128)S(1)}, u32[]{:S(2)}, u32[]{:S(2)}) collective-permute-start(f32[320,128]{1,0:T(8,128)S(1)} %get-tuple-element.11), channel_id=1, source_target_pairs={{0,1},{1,0},{2,3},{3,2},{4,5},{5,4},{6,7},{7,6},{8,9},{9,8},{10,11... | collective-permute-start | bytes 491528 | tf_op jit(solution)/shard_map/ppermute | solution.py:287

commit v7 on v6

--- a/solution.py
+++ b/solution.py
@@ -148,7 +148,7 @@
         at, row = k // 8, k % 8
         first, second = ahead.pop(k), ahead.pop(k + 1)
         up = lambda x: pltpu.roll(x, 7, 0)
-        a, b, d = first[at], second[at], up(second[at])
+        a, b, d = first[at], up(first[at]), up(second[at])
         inverse = 1.0 / (a * d - b * b)
         p, q, r = (x[row : row + 1, :] for x in (d * inverse, b * inverse, a * inverse))
 
@@ -184,7 +184,8 @@
 
 
 def solve_kernel(sums_ref, stack_ref, update_hbm, residual_hbm, update_ref, residual_ref, update_sem, residual_sem):
-    u = [sums_ref[64 * k : 64 * (k + 1), :] for k in range(7)]
+    place = lambda k, i: 128 * (k // 2) + 16 * i + 8 * (k % 2)
+    u = [jnp.concatenate([sums_ref[place(k, i) : place(k, i) + 8, :] for i in range(8)], axis=0) for k in range(7)]
     row = lax.broadcasted_iota(jnp.int32, (BS, 128), 0)
     lane = lax.broadcasted_iota(jnp.int32, (BS, 128), 1)
     eye = jnp.where(row == lane % BS, 1.0, 0.0)
@@ -276,7 +277,6 @@
 
 
 AXES = ("y", "z", "next", "x", "core")
-NEAR = ("y", "next", "x", "core")
 
 
 def shards(right_side, blocks, cols):
@@ -286,9 +286,9 @@
     other = lax.ppermute(other, AXES, [(i, ((i - 1) ^ 1) + 1) if 0 < i < devices - 1 else (i, devices - 1 - i) for i in range(devices)])
     pair = lax.ppermute(pair, AXES, [(i, i ^ 1) for i in range(devices)])
     sums, stack = basis(flag, own, other, pair)
-    parts = lax.all_to_all(sums.reshape(64, 8, 128), NEAR, 0, 0)
-    parts = lax.all_to_all(total(parts, 8), "z", 0, 0)
-    sums = lax.all_to_all(total(parts, 64), NEAR, 0, 0)
+    parts = lax.all_to_all(sums.reshape(64, 8, 128), ("y", "next", "x", "core"), 0, 0)
+    parts = lax.all_to_all(total(parts, 16), ("z", "next"), 0, 0)
+    sums = lax.all_to_all(total(parts.reshape(8, 16, 128), 32), ("y", "x", "core"), 0, 0)
     return tuple(solve(sums.reshape(512, 128), stack))
 
 

time: 80.4 us -> 78.8 us (0.980)
  blocking collectives: 49.3 us -> 47.9 us
    all_to_all x3, blocking collectives: 49.3 us -> 47.9 us  [the longest x1 20.2 us: shards(): parts = lax.all_to_all(total(parts, 16), ('z', 'next'), 0, 0)]
where the time goes in v7:
time: 78.8 us; the launch traced here: 78.5 us
  blocking collectives  47.9 us (61%)
  starting transfers between devices  18.9 us (24%)
  Pallas kernels  10 us (13%)
  waiting for transfers between devices  1 us (1%)
    all_to_all x1, blocking collectives, shards(): parts = lax.all_to_all(total(parts, 16), ('z', 'next'), 0, 0)  20.2 us
    ppermute x1, starting transfers between devices, shards(): pair = lax.ppermute(pair, AXES, [(i, i ^ 1) for i in range(devices)])  14.4 us
    all_to_all x1, blocking collectives, shards(): lax.all_to_all(total(parts.reshape(8, 16, 128), 32), ('y', 'x', 'core'),...  14.3 us
    all_to_all x1, blocking collectives, shards(): lax.all_to_all(sums.reshape(64, 8, 128), ('y', 'next', 'x', 'core'), 0, 0)  13.5 us
    pallas_call x1, Pallas kernels, solve(): call(solve_kernel, [(64, 256), (64, 256)], [VMEM, VMEM], scratch, 'solve'...  6.87 us
    ppermute x1, starting transfers between devices, shards(): lax.ppermute(other, AXES, [(i, (i - 1 ^ 1) + 1) if 0 < i < devices - 1 el...  4.5 us
    pallas_call x1, Pallas kernels, basis(): call(basis_kernel, [(512, 128), (256, 512)], [VMEM] * 4, name='basis')  1.62 us
  transfers between devices with their start and end apart: 2, of which 1 were waited for; matrix products, arithmetic and copies ran while one was open for 0% of the time, Pallas kernels for 0%

profile of v7, /device:TPU:1, one launch (start us, length us, event | category | flops | bytes accessed | tf_op | source)
XLA Modules:
  0.0 78.5 jit_solution(7816723712368431718)
XLA Ops:
  0.6 1.4 %pack.1 = (f32[256,256]{1,0:T(8,128)S(1)}, f32[320,128]{1,0:T(8,128)S(1)}, f32[320,128]{1,0:T(8,128)S(1)}, f32[8,128]{1,0:T(8,128)S(1)}) custom-call(s32[4,7]{1,0:T(4,128)} %bitcast.7, f32[64,256]{1,0:T(8,128)} %right_ref.1, f32[7,64,256]{2,1,0:T(8,128)} %blocks_ref.1), custom_call_target="tpu_custom_call" | custom-call | tf_op jit(solution)/shard_map/pack/pallas_call | solution.py:262
  2.1 4.5 %collective-permute-start = (f32[320,128]{1,0:T(8,128)S(1)}, f32[320,128]{1,0:T(8,128)S(1)}, u32[]{:S(2)}, u32[]{:S(2)}) collective-permute-start(f32[320,128]{1,0:T(8,128)S(1)} %get-tuple-element.10), channel_id=1, source_target_pairs={{0,511},{1,2},{2,1},{3,4},{4,3},{5,6},{6,5},{7,8},{8,7},{9,10},{10... | collective-permute-start | bytes 491528 | tf_op jit(solution)/shard_map/ppermute | solution.py:286
  6.6 14.4 %collective-permute-start.1 = (f32[320,128]{1,0:T(8,128)S(1)}, f32[320,128]{1,0:T(8,128)S(1)}, u32[]{:S(2)}, u32[]{:S(2)}) collective-permute-start(f32[320,128]{1,0:T(8,128)S(1)} %get-tuple-element.11), channel_id=1, source_target_pairs={{0,1},{1,0},{2,3},{3,2},{4,5},{5,4},{6,7},{7,6},{8,9},{9,8},{10,11... | collective-permute-start | bytes 491528 | tf_op jit(solution)/shard_map/ppermute | solution.py:287
  21.0 0.0 collective-permute-done.other_ref
  21.0 1.0 %collective-permute-done.1.pair_ref = f32[320,128]{1,0:T(8,128)S(1)} collective-permute-done((f32[320,128]{1,0:T(8,128)S(1)}, f32[320,128]{1,0:T(8,128)S(1)}, u32[]{:S(2)}, u32[]{:S(2)}) %collective-permute-start.1) | collective-permute-done | bytes 163872 | tf_op jit(solution)/shard_map/ppermute | solution.py:287
  22.0 1.6 %basis.1 = (f32[512,128]{1,0:T(8,128)S(1)}, f32[256,512]{1,0:T(8,128)S(1)}) custom-call(f32[8,128]{1,0:T(8,128)S(1)} %get-tuple-element.8.flag_ref, f32[256,256]{1,0:T(8,128)S(1)} %get-tuple-element.9.own_ref, f32[320,128]{1,0:T(8,128)S(1)} %collective-permute-done.other_ref, f32[320,128]{1,0:T(8,128)S(1)} %collective-permute-done.1.pair_ref), custom_call_target="tpu_custom_call" | custom-call | tf_op jit(solution)/shard_map/basis/pallas_call | solution.py:266
  23.6 13.5 %all_to_all.15.in_ref = f32[64,8,128]{2,1,0:T(8,128)S(1)} all-to-all(f32[64,8,128]{2,1,0:T(8,128)S(1)} %bitcast.6), channel_id=1, replica_groups=mesh['y'=4,'z'=8,'next'=2,'x'=4,'core'=2] {'y','next','x','core'}, dimensions={0} | all-to-all | bytes 524288 | tf_op jit(solution)/shard_map/all_to_all | solution.py:289
  37.1 0.1 total.2
  37.2 20.2 %all_to_all.16 = f32[16,8,128]{2,1,0:T(8,128)S(1)} all-to-all(f32[16,8,128]{2,1,0:T(8,128)S(1)} %total.2), channel_id=1, replica_groups=mesh['y'=4,'z'=8,'next'=2,'x'=4,'core'=2] {'z','next'}, dimensions={0} | all-to-all | bytes 131072 | tf_op jit(solution)/shard_map/all_to_all | solution.py:290
  57.4 14.3 %all_to_all.17 = f32[32,16,128]{2,1,0:T(8,128)S(1)} all-to-all(f32[32,16,128]{2,1,0:T(8,128)S(1)} %total.3), channel_id=1, replica_groups=mesh['y'=4,'z'=8,'next'=2,'x'=4,'core'=2] {'y','x','core'}, dimensions={0} | all-to-all | bytes 524288 | tf_op jit(solution)/shard_map/all_to_all | solution.py:291
  71.6 6.9 %solve.1 = (f32[64,256]{1,0:T(8,128)}, f32[64,256]{1,0:T(8,128)}) custom-call(f32[512,128]{1,0:T(8,128)S(1)} %bitcast.4, f32[256,512]{1,0:T(8,128)S(1)} %get-tuple-element.13.stack_ref), custom_call_target="tpu_custom_call" | custom-call | tf_op jit(solution)/shard_map/solve/pallas_call | solution.py:276
  (1 shorter events, 0.0 us)
Async XLA Ops:
  2.1 18.9 %collective-permute-start = (f32[320,128]{1,0:T(8,128)S(1)}, f32[320,128]{1,0:T(8,128)S(1)}, u32[]{:S(2)}, u32[]{:S(2)}) collective-permute-start(f32[320,128]{1,0:T(8,128)S(1)} %get-tuple-element.10), channel_id=1, source_target_pairs={{0,511},{1,2},{2,1},{3,4},{4,3},{5,6},{6,5},{7,8},{8,7},{9,10},{10... | collective-permute-start | bytes 491528 | tf_op jit(solution)/shard_map/ppermute | solution.py:286
  6.6 15.4 %collective-permute-start.1 = (f32[320,128]{1,0:T(8,128)S(1)}, f32[320,128]{1,0:T(8,128)S(1)}, u32[]{:S(2)}, u32[]{:S(2)}) collective-permute-start(f32[320,128]{1,0:T(8,128)S(1)} %get-tuple-element.11), channel_id=1, source_target_pairs={{0,1},{1,0},{2,3},{3,2},{4,5},{5,4},{6,7},{7,6},{8,9},{9,8},{10,11... | collective-permute-start | bytes 491528 | tf_op jit(solution)/shard_map/ppermute | solution.py:287

commit v8 on v5

--- a/solution.py
+++ b/solution.py
@@ -148,7 +148,7 @@
         at, row = k // 8, k % 8
         first, second = ahead.pop(k), ahead.pop(k + 1)
         up = lambda x: pltpu.roll(x, 7, 0)
-        a, b, d = first[at], second[at], up(second[at])
+        a, b, d = first[at], up(first[at]), up(second[at])
         inverse = 1.0 / (a * d - b * b)
         p, q, r = (x[row : row + 1, :] for x in (d * inverse, b * inverse, a * inverse))
 

time: 78.3 us -> 78.1 us (level)
  no operation moved by 1% of the time
where the time goes in v8:
time: 78.1 us; the launch traced here: 77.8 us
  blocking collectives  47.2 us (60%)
  starting transfers between devices  18.9 us (24%)
  Pallas kernels  9.99 us (13%)
  waiting for transfers between devices  1 us (1%)
    all_to_all x1, blocking collectives, shards(): parts = lax.all_to_all(total(parts, 16), 'z', 0, 0)  20.1 us
    all_to_all x1, blocking collectives, shards(): sums = lax.all_to_all(total(parts, 32), PLANE, 0, 0)  15.1 us
    ppermute x1, starting transfers between devices, shards(): pair = lax.ppermute(pair, AXES, [(i, i ^ 1) for i in range(devices)])  14.4 us
    all_to_all x1, blocking collectives, shards(): parts = lax.all_to_all(sums.reshape(32, 16, 128), PLANE, 0, 0)  12 us
    pallas_call x1, Pallas kernels, solve(): call(solve_kernel, [(64, 256), (64, 256)], [VMEM, VMEM], scratch, 'solve'...  6.88 us
    ppermute x1, starting transfers between devices, shards(): lax.ppermute(other, AXES, [(i, (i - 1 ^ 1) + 1) if 0 < i < devices - 1 el...  4.5 us
    pallas_call x1, Pallas kernels, basis(): call(basis_kernel, [(512, 128), (256, 512)], [VMEM] * 4, name='basis')  1.62 us
  transfers between devices with their start and end apart: 2, of which 1 were waited for; matrix products, arithmetic and copies ran while one was open for 0% of the time, Pallas kernels for 0%

profile of v8, /device:TPU:1, one launch (start us, length us, event | category | flops | bytes accessed | tf_op | source)
XLA Modules:
  0.0 77.8 jit_solution(18406131030587930187)
XLA Ops:
  0.6 1.4 %pack.1 = (f32[256,256]{1,0:T(8,128)S(1)}, f32[320,128]{1,0:T(8,128)S(1)}, f32[320,128]{1,0:T(8,128)S(1)}, f32[8,128]{1,0:T(8,128)S(1)}) custom-call(s32[4,7]{1,0:T(4,128)} %bitcast.5, f32[64,256]{1,0:T(8,128)} %right_ref.1, f32[7,64,256]{2,1,0:T(8,128)} %blocks_ref.1), custom_call_target="tpu_custom_call" | custom-call | tf_op jit(solution)/shard_map/pack/pallas_call | solution.py:261
  2.1 4.5 %collective-permute-start = (f32[320,128]{1,0:T(8,128)S(1)}, f32[320,128]{1,0:T(8,128)S(1)}, u32[]{:S(2)}, u32[]{:S(2)}) collective-permute-start(f32[320,128]{1,0:T(8,128)S(1)} %get-tuple-element.10), channel_id=1, source_target_pairs={{0,511},{1,2},{2,1},{3,4},{4,3},{5,6},{6,5},{7,8},{8,7},{9,10},{10... | collective-permute-start | bytes 491528 | tf_op jit(solution)/shard_map/ppermute | solution.py:286
  6.6 14.4 %collective-permute-start.1 = (f32[320,128]{1,0:T(8,128)S(1)}, f32[320,128]{1,0:T(8,128)S(1)}, u32[]{:S(2)}, u32[]{:S(2)}) collective-permute-start(f32[320,128]{1,0:T(8,128)S(1)} %get-tuple-element.11), channel_id=1, source_target_pairs={{0,1},{1,0},{2,3},{3,2},{4,5},{5,4},{6,7},{7,6},{8,9},{9,8},{10,11... | collective-permute-start | bytes 491528 | tf_op jit(solution)/shard_map/ppermute | solution.py:287
  21.0 0.0 collective-permute-done.other_ref
  21.0 1.0 %collective-permute-done.1.pair_ref = f32[320,128]{1,0:T(8,128)S(1)} collective-permute-done((f32[320,128]{1,0:T(8,128)S(1)}, f32[320,128]{1,0:T(8,128)S(1)}, u32[]{:S(2)}, u32[]{:S(2)}) %collective-permute-start.1) | collective-permute-done | bytes 163872 | tf_op jit(solution)/shard_map/ppermute | solution.py:287
  22.0 1.6 %basis.1 = (f32[512,128]{1,0:T(8,128)S(1)}, f32[256,512]{1,0:T(8,128)S(1)}) custom-call(f32[8,128]{1,0:T(8,128)S(1)} %get-tuple-element.8.flag_ref, f32[256,256]{1,0:T(8,128)S(1)} %get-tuple-element.9.own_ref, f32[320,128]{1,0:T(8,128)S(1)} %collective-permute-done.other_ref, f32[320,128]{1,0:T(8,128)S(1)} %collective-permute-done.1.pair_ref), custom_call_target="tpu_custom_call" | custom-call | tf_op jit(solution)/shard_map/basis/pallas_call | solution.py:265
  23.6 12.0 %all_to_all.15.in_ref = f32[32,16,128]{2,1,0:T(8,128)S(1)} all-to-all(f32[32,16,128]{2,1,0:T(8,128)S(1)} %bitcast.4), channel_id=1, replica_groups=mesh['y'=4,'z'=16,'x'=4,'core'=2] {'y','x','core'}, dimensions={0} | all-to-all | bytes 524288 | tf_op jit(solution)/shard_map/all_to_all | solution.py:289
  35.6 20.1 %all_to_all.16.in_ref = f32[16,16,128]{2,1,0:T(8,128)S(1)} all-to-all(f32[16,16,128]{2,1,0:T(8,128)S(1)} %total.2), channel_id=1, replica_groups=mesh['y'=4,'z'=16,'x'=4,'core'=2] {'z'}, dimensions={0} | all-to-all | bytes 262144 | tf_op jit(solution)/shard_map/all_to_all | solution.py:290
  55.8 15.1 %all_to_all.17 = f32[32,16,128]{2,1,0:T(8,128)S(1)} all-to-all(f32[32,16,128]{2,1,0:T(8,128)S(1)} %total.3), channel_id=1, replica_groups=mesh['y'=4,'z'=16,'x'=4,'core'=2] {'y','x','core'}, dimensions={0} | all-to-all | bytes 524288 | tf_op jit(solution)/shard_map/all_to_all | solution.py:291
  70.9 6.9 %solve.1 = (f32[64,256]{1,0:T(8,128)}, f32[64,256]{1,0:T(8,128)}) custom-call(f32[512,128]{1,0:T(8,128)S(1)} %bitcast.3, f32[256,512]{1,0:T(8,128)S(1)} %get-tuple-element.13.stack_ref), custom_call_target="tpu_custom_call" | custom-call | tf_op jit(solution)/shard_map/solve/pallas_call | solution.py:275
  (2 shorter events, 0.1 us)
Async XLA Ops:
  2.1 18.9 %collective-permute-start = (f32[320,128]{1,0:T(8,128)S(1)}, f32[320,128]{1,0:T(8,128)S(1)}, u32[]{:S(2)}, u32[]{:S(2)}) collective-permute-start(f32[320,128]{1,0:T(8,128)S(1)} %get-tuple-element.10), channel_id=1, source_target_pairs={{0,511},{1,2},{2,1},{3,4},{4,3},{5,6},{6,5},{7,8},{8,7},{9,10},{10... | collective-permute-start | bytes 491528 | tf_op jit(solution)/shard_map/ppermute | solution.py:286
  6.6 15.4 %collective-permute-start.1 = (f32[320,128]{1,0:T(8,128)S(1)}, f32[320,128]{1,0:T(8,128)S(1)}, u32[]{:S(2)}, u32[]{:S(2)}) collective-permute-start(f32[320,128]{1,0:T(8,128)S(1)} %get-tuple-element.11), channel_id=1, source_target_pairs={{0,1},{1,0},{2,3},{3,2},{4,5},{5,4},{6,7},{7,6},{8,9},{9,8},{10,11... | collective-permute-start | bytes 491528 | tf_op jit(solution)/shard_map/ppermute | solution.py:287

commit v9 on v8

--- a/solution.py
+++ b/solution.py
@@ -168,12 +168,12 @@
             top, low = solved(column[at])
             for g in live:
                 if g in column:
-                    column[g] = column[g] - (first[g] * top + second[g] * low)
+                    column[g] = column[g] - first[g] * top - second[g] * low
         for t in range(tiles):
             top, low = solved(part[at][t])
             n = top.shape[1]
             for g in live:
-                part[g][t] = part[g][t] - (first[g][:, :n] * top + second[g][:, :n] * low)
+                part[g][t] = part[g][t] - first[g][:, :n] * top - second[g][:, :n] * low
             pair = jnp.where(rows == row, top, low)
             scaled[at][t] = pair if row == 0 else jnp.where(rows < row, scaled[at][t], pair)
         for late in (k + 2 * WINDOW, k + 2 * WINDOW + 1):

time: 78.1 us -> 78.3 us (level)
  no operation moved by 1% of the time
where the time goes in v9:
time: 78.3 us; the launch traced here: 78 us
  blocking collectives  47.2 us (60%)
  starting transfers between devices  18.9 us (24%)
  Pallas kernels  10.2 us (13%)
  waiting for transfers between devices  1 us (1%)
    all_to_all x1, blocking collectives, shards(): parts = lax.all_to_all(total(parts, 16), 'z', 0, 0)  20.1 us
    all_to_all x1, blocking collectives, shards(): sums = lax.all_to_all(total(parts, 32), PLANE, 0, 0)  15.1 us
    ppermute x1, starting transfers between devices, shards(): pair = lax.ppermute(pair, AXES, [(i, i ^ 1) for i in range(devices)])  14.4 us
    all_to_all x1, blocking collectives, shards(): parts = lax.all_to_all(sums.reshape(32, 16, 128), PLANE, 0, 0)  12 us
    pallas_call x1, Pallas kernels, solve(): call(solve_kernel, [(64, 256), (64, 256)], [VMEM, VMEM], scratch, 'solve'...  7.07 us
    ppermute x1, starting transfers between devices, shards(): lax.ppermute(other, AXES, [(i, (i - 1 ^ 1) + 1) if 0 < i < devices - 1 el...  4.5 us
    pallas_call x1, Pallas kernels, basis(): call(basis_kernel, [(512, 128), (256, 512)], [VMEM] * 4, name='basis')  1.62 us
  transfers between devices with their start and end apart: 2, of which 1 were waited for; matrix products, arithmetic and copies ran while one was open for 0% of the time, Pallas kernels for 0%

profile of v9, /device:TPU:1, one launch (start us, length us, event | category | flops | bytes accessed | tf_op | source)
XLA Modules:
  0.0 78.0 jit_solution(16326432070096998574)
XLA Ops:
  0.6 1.4 %pack.1 = (f32[256,256]{1,0:T(8,128)S(1)}, f32[320,128]{1,0:T(8,128)S(1)}, f32[320,128]{1,0:T(8,128)S(1)}, f32[8,128]{1,0:T(8,128)S(1)}) custom-call(s32[4,7]{1,0:T(4,128)} %bitcast.5, f32[64,256]{1,0:T(8,128)} %right_ref.1, f32[7,64,256]{2,1,0:T(8,128)} %blocks_ref.1), custom_call_target="tpu_custom_call" | custom-call | tf_op jit(solution)/shard_map/pack/pallas_call | solution.py:261
  2.1 4.5 %collective-permute-start = (f32[320,128]{1,0:T(8,128)S(1)}, f32[320,128]{1,0:T(8,128)S(1)}, u32[]{:S(2)}, u32[]{:S(2)}) collective-permute-start(f32[320,128]{1,0:T(8,128)S(1)} %get-tuple-element.10), channel_id=1, source_target_pairs={{0,511},{1,2},{2,1},{3,4},{4,3},{5,6},{6,5},{7,8},{8,7},{9,10},{10... | collective-permute-start | bytes 491528 | tf_op jit(solution)/shard_map/ppermute | solution.py:286
  6.6 14.4 %collective-permute-start.1 = (f32[320,128]{1,0:T(8,128)S(1)}, f32[320,128]{1,0:T(8,128)S(1)}, u32[]{:S(2)}, u32[]{:S(2)}) collective-permute-start(f32[320,128]{1,0:T(8,128)S(1)} %get-tuple-element.11), channel_id=1, source_target_pairs={{0,1},{1,0},{2,3},{3,2},{4,5},{5,4},{6,7},{7,6},{8,9},{9,8},{10,11... | collective-permute-start | bytes 491528 | tf_op jit(solution)/shard_map/ppermute | solution.py:287
  21.0 0.0 collective-permute-done.other_ref
  21.0 1.0 %collective-permute-done.1.pair_ref = f32[320,128]{1,0:T(8,128)S(1)} collective-permute-done((f32[320,128]{1,0:T(8,128)S(1)}, f32[320,128]{1,0:T(8,128)S(1)}, u32[]{:S(2)}, u32[]{:S(2)}) %collective-permute-start.1) | collective-permute-done | bytes 163872 | tf_op jit(solution)/shard_map/ppermute | solution.py:287
  22.0 1.6 %basis.1 = (f32[512,128]{1,0:T(8,128)S(1)}, f32[256,512]{1,0:T(8,128)S(1)}) custom-call(f32[8,128]{1,0:T(8,128)S(1)} %get-tuple-element.8.flag_ref, f32[256,256]{1,0:T(8,128)S(1)} %get-tuple-element.9.own_ref, f32[320,128]{1,0:T(8,128)S(1)} %collective-permute-done.other_ref, f32[320,128]{1,0:T(8,128)S(1)} %collective-permute-done.1.pair_ref), custom_call_target="tpu_custom_call" | custom-call | tf_op jit(solution)/shard_map/basis/pallas_call | solution.py:265
  23.6 12.0 %all_to_all.15.in_ref = f32[32,16,128]{2,1,0:T(8,128)S(1)} all-to-all(f32[32,16,128]{2,1,0:T(8,128)S(1)} %bitcast.4), channel_id=1, replica_groups=mesh['y'=4,'z'=16,'x'=4,'core'=2] {'y','x','core'}, dimensions={0} | all-to-all | bytes 524288 | tf_op jit(solution)/shard_map/all_to_all | solution.py:289
  35.6 20.1 %all_to_all.16.in_ref = f32[16,16,128]{2,1,0:T(8,128)S(1)} all-to-all(f32[16,16,128]{2,1,0:T(8,128)S(1)} %total.2), channel_id=1, replica_groups=mesh['y'=4,'z'=16,'x'=4,'core'=2] {'z'}, dimensions={0} | all-to-all | bytes 262144 | tf_op jit(solution)/shard_map/all_to_all | solution.py:290
  55.8 15.1 %all_to_all.17 = f32[32,16,128]{2,1,0:T(8,128)S(1)} all-to-all(f32[32,16,128]{2,1,0:T(8,128)S(1)} %total.3), channel_id=1, replica_groups=mesh['y'=4,'z'=16,'x'=4,'core'=2] {'y','x','core'}, dimensions={0} | all-to-all | bytes 524288 | tf_op jit(solution)/shard_map/all_to_all | solution.py:291
  70.9 7.1 %solve.1 = (f32[64,256]{1,0:T(8,128)}, f32[64,256]{1,0:T(8,128)}) custom-call(f32[512,128]{1,0:T(8,128)S(1)} %bitcast.3, f32[256,512]{1,0:T(8,128)S(1)} %get-tuple-element.13.stack_ref), custom_call_target="tpu_custom_call" | custom-call | tf_op jit(solution)/shard_map/solve/pallas_call | solution.py:275
  (2 shorter events, 0.1 us)
Async XLA Ops:
  2.1 18.9 %collective-permute-start = (f32[320,128]{1,0:T(8,128)S(1)}, f32[320,128]{1,0:T(8,128)S(1)}, u32[]{:S(2)}, u32[]{:S(2)}) collective-permute-start(f32[320,128]{1,0:T(8,128)S(1)} %get-tuple-element.10), channel_id=1, source_target_pairs={{0,511},{1,2},{2,1},{3,4},{4,3},{5,6},{6,5},{7,8},{8,7},{9,10},{10... | collective-permute-start | bytes 491528 | tf_op jit(solution)/shard_map/ppermute | solution.py:286
  6.6 15.4 %collective-permute-start.1 = (f32[320,128]{1,0:T(8,128)S(1)}, f32[320,128]{1,0:T(8,128)S(1)}, u32[]{:S(2)}, u32[]{:S(2)}) collective-permute-start(f32[320,128]{1,0:T(8,128)S(1)} %get-tuple-element.11), channel_id=1, source_target_pairs={{0,1},{1,0},{2,3},{3,2},{4,5},{5,4},{6,7},{7,6},{8,9},{9,8},{10,11... | collective-permute-start | bytes 491528 | tf_op jit(solution)/shard_map/ppermute | solution.py:287
